TPU v7x, 32 devices: a whole 2x2x4 slice. The times are simulated.
32 devices in a mesh: section: 2 (over x), gy: 4 (over y, core), gx: 4 (over z).
Axes of the slice: x: 2, y: 2, z: 4, core: 2. Of those that a mesh axis runs over, the one named last changes fastest.
Arguments:
- images: bfloat16 [2, 128, 256, 128], P('section', 'gy', 'gx'), may hold values from -6 to 6
- first_kernel: bfloat16 [3, 3, 128, 128], replicated, may hold values from -0.1875 to 0.1875
- projection: bfloat16 [128, 256], replicated, may hold values from -0.5 to 0.5
- second_kernel: bfloat16 [3, 3, 256, 256], replicated, may hold values from -0.125 to 0.125
- cotangent: bfloat16 [2, 64, 128, 256], P('section', 'gy', 'gx'), may hold values from -0.625 to 0.625
Outputs:
- features: bfloat16 [2, 64, 128, 256], P('section', 'gy', 'gx')
- grad_first: float32 [3, 3, 128, 128], replicated
- grad_projection: float32 [128, 256], replicated
- grad_second: float32 [3, 3, 256, 256], replicated
All inputs are finite; a program needn't handle non-finite values.
Results may differ from a plain program's by a relative error of at most 0.014.
Values may be sent and summed in bfloat16 or wider, within the bound.
No kernel may reach another device: no remote copies, remote signals or barrier semaphores. Data moves between devices by JAX's collectives and lax.ppermute only.
A program may use at most 64 MiB of HBM per device.

v0:
```python
import jax
import jax.numpy as jnp
from jax import lax
from jax.sharding import PartitionSpec as P


def padded_2(array, sides, width):
    for axis, dim in sides:
        size, length = (lax.axis_size(axis), array.shape[dim])
        up = [(i, (i + 1) % size) for i in range(size - 1)]
        down = [(j, i) for i, j in up]
        last = lax.slice_in_dim(array, length - width, length, axis=dim)
        initial = lax.slice_in_dim(array, 0, width, axis=dim)
        before = lax.ppermute(last, axis, up)
        after = lax.ppermute(initial, axis, down)
        array = jnp.concatenate([before, array, after], axis=dim)
    return array


def from_partner(block, axis, bit):
    count = lax.axis_size(axis)
    route = []
    for low in range(count):
        high = low | 1 << bit
        if high != low and high < count:
            route += [(low, high), (high, low)]
    return lax.ppermute(block, axis, route)


def silu_slope(values):
    sigma = jax.nn.sigmoid(values)
    return sigma * (1.0 + values * (1.0 - sigma))


def conv_forward(padded, kernel, row_count, col_count):
    total = jnp.zeros((row_count * col_count, kernel.shape[3]), jnp.float32)
    for row_tap in range(3):
        for col_tap in range(3):
            piece = padded[row_tap : row_tap + row_count, col_tap : col_tap + col_count].reshape(
                row_count * col_count, padded.shape[2]
            )
            total = total + jnp.dot(
                piece, kernel[row_tap, col_tap], preferred_element_type=jnp.float32
            )
    return total


def conv_slopes(padded, slope, row_count, col_count):
    pieces = []
    for row_tap in range(3):
        for col_tap in range(3):
            piece = padded[row_tap : row_tap + row_count, col_tap : col_tap + col_count].reshape(
                row_count * col_count, padded.shape[2]
            )
            pieces.append(jnp.einsum("pc,pd->cd", piece, slope, preferred_element_type=jnp.float32))
    return jnp.stack(pieces).reshape(3, 3, padded.shape[2], slope.shape[1])


def conv_back(padded, kernel, row_count, col_count):
    total = jnp.zeros((row_count * col_count, kernel.shape[2]), jnp.float32)
    for row_tap in range(3):
        for col_tap in range(3):
            piece = padded[
                2 - row_tap : 2 - row_tap + row_count, 2 - col_tap : 2 - col_tap + col_count
            ].reshape(row_count * col_count, padded.shape[2])
            total = total + jnp.einsum(
                "pd,cd->pc", piece, kernel[row_tap, col_tap], preferred_element_type=jnp.float32
            )
    return total


def first_forward(tile, first_kernel):
    row_count, col_count, channels = tile.shape
    padded = padded_2(tile, (("gy", 0), ("gx", 1)), 1)
    before = conv_forward(padded, first_kernel, row_count, col_count)
    hidden = jax.nn.silu(before).astype(jnp.bfloat16).reshape(row_count, col_count, channels)
    pooled = (
        hidden.astype(jnp.float32)
        .reshape(row_count // 2, 2, col_count // 2, 2, channels)
        .sum(axis=(1, 3))
        * 0.25
    ).astype(jnp.bfloat16)
    return (padded, before, pooled)


def project(pooled, projection):
    half_rows, half_cols, channels = pooled.shape
    flat = jnp.dot(
        pooled.reshape(half_rows * half_cols, channels),
        projection,
        preferred_element_type=jnp.float32,
    )
    return flat.astype(jnp.bfloat16).reshape(half_rows, half_cols, projection.shape[1])


def second_pass(middle, second_kernel, upstream):
    half_rows, half_cols, wide = middle.shape
    padded = padded_2(middle, (("gy", 0), ("gx", 1)), 1)
    before = conv_forward(padded, second_kernel, half_rows, half_cols)
    output = jax.nn.silu(before).astype(jnp.bfloat16).reshape(half_rows, half_cols, wide)
    flat_up = upstream.reshape(half_rows * half_cols, wide).astype(jnp.float32)
    slope = (flat_up * silu_slope(before)).astype(jnp.bfloat16)
    kernel_grad = conv_slopes(padded, slope, half_rows, half_cols)
    slope_padded = padded_2(slope.reshape(half_rows, half_cols, wide), (("gy", 0), ("gx", 1)), 1)
    back = conv_back(slope_padded, second_kernel, half_rows, half_cols).astype(jnp.bfloat16)
    return (output, kernel_grad, back.reshape(half_rows, half_cols, wide))


def projection_back(pooled, back, projection):
    half_rows, half_cols, channels = pooled.shape
    flat_pool = pooled.reshape(half_rows * half_cols, channels)
    flat_back = back.reshape(half_rows * half_cols, back.shape[2])
    grad = jnp.einsum("pc,pd->cd", flat_pool, flat_back, preferred_element_type=jnp.float32)
    pooled_slope = jnp.einsum(
        "pd,cd->pc", flat_back, projection, preferred_element_type=jnp.float32
    )
    return (grad, pooled_slope.astype(jnp.bfloat16).reshape(half_rows, half_cols, channels))


def first_back(padded, before, pooled_slope):
    half_rows, half_cols, channels = pooled_slope.shape
    spread = jnp.broadcast_to(
        (pooled_slope.astype(jnp.float32) * 0.25)[:, None, :, None, :],
        (half_rows, 2, half_cols, 2, channels),
    )
    spread = spread.reshape(4 * half_rows * half_cols, channels)
    slope = (spread * silu_slope(before)).astype(jnp.bfloat16)
    return conv_slopes(padded, slope, 2 * half_rows, 2 * half_cols)


def per_device(images, first_kernel, projection, second_kernel, cotangent):
    padded, before, pooled = first_forward(images[0], first_kernel)
    upstream = from_partner(cotangent[0], "section", 0)
    middle = project(pooled, projection)
    output, grad_second, back = second_pass(middle, second_kernel, upstream)
    grad_projection, pooled_slope = projection_back(pooled, back, projection)
    output = from_partner(output, "section", 0)
    grad_first = first_back(padded, before, pooled_slope)
    grad_first, grad_projection, grad_second = lax.psum(
        (grad_first, grad_projection, grad_second), ("section", "gy", "gx")
    )
    return (output[None], grad_first, grad_projection, grad_second)


def solution(mesh):
    placed = (P("section", "gy", "gx", None), P(), P(), P(), P("section", "gy", "gx", None))
    return jax.shard_map(
        per_device,
        mesh=mesh,
        in_specs=placed,
        out_specs=(P("section", "gy", "gx", None), P(), P(), P()),
        check_vma=False,
    )
```

profile of v0, /device:TPU:0, one launch (start us, length us, event | category | flops | bytes accessed | tf_op | source)
XLA Modules:
  0.0 227.4 jit_solution(3787896188777336523)
XLA Ops:
  8.0 2.4 %collective-permute-start = (bf16[1,64,128]{2,1,0:T(8,128)(2,1)S(1)}, bf16[1,64,128]{2,1,0:T(8,128)(2,1)S(1)}, u32[]{:S(2)}, u32[]{:S(2)}) collective-permute-start(bf16[1,64,128]{2,1,0:T(8,128)(2,1)S(1)} %get-tuple-element.21), channel_id=1, source_target_pairs={{0,4},{4,8},{8,12},{1,5},{5,9},{9,13},{2,6},{6,10},{10,14},{3,7},{... | collective-permute-start | bytes 49160 | tf_op jit(solution)/shard_map/ppermute | solution.py:14
  10.4 1.3 collective-permute-start.1
  11.7 3.9 %collective-permute-done.1 = bf16[1,64,128]{2,1,0:T(8,128)(2,1)S(1)} collective-permute-done((bf16[1,64,128]{2,1,0:T(8,128)(2,1)S(1)}, bf16[1,64,128]{2,1,0:T(8,128)(2,1)S(1)}, u32[]{:S(2)}, u32[]{:S(2)}) %collective-permute-start.1) | collective-permute-done | bytes 16416 | tf_op jit(solution)/shard_map/ppermute | solution.py:15
  16.5 3.5 %collective-permute-start.2 = (bf16[34,1,128]{2,1,0:T(2,128)(2,1)S(1)}, bf16[34,1,128]{2,1,0:T(2,128)(2,1)S(1)}, u32[]{:S(2)}, u32[]{:S(2)}) collective-permute-start(bf16[34,1,128]{2,1,0:T(2,128)(2,1)S(1)} %get-tuple-element.15), channel_id=1, source_target_pairs={{0,1},{1,2},{2,3},{4,5},{5,6},{6,7},{8,9},{9,10},{10,11},{12,13},{... | collective-permute-start | bytes 26120 | tf_op jit(solution)/shard_map/ppermute | solution.py:14
  20.0 1.4 collective-permute-start.3
  21.5 1.3 pad_maximum_fusion.1
  23.1 2.8 %collective-permute-done.3 = bf16[34,1,128]{2,1,0:T(2,128)(2,1)S(1)} collective-permute-done((bf16[34,1,128]{2,1,0:T(2,128)(2,1)S(1)}, bf16[34,1,128]{2,1,0:T(2,128)(2,1)S(1)}, u32[]{:S(2)}, u32[]{:S(2)}) %collective-permute-start.3) | collective-permute-done | bytes 8736 | tf_op jit(solution)/shard_map/ppermute | solution.py:15
  30.4 3.0 %collective-permute-start.4 = (bf16[1,32,256]{2,1,0:T(8,128)(2,1)S(1)}, bf16[1,32,256]{2,1,0:T(8,128)(2,1)S(1)}, u32[]{:S(2)}, u32[]{:S(2)}) collective-permute-start(bf16[1,32,256]{2,1,0:T(8,128)(2,1)S(1)} %get-tuple-element.49), channel_id=1, source_target_pairs={{0,4},{4,8},{8,12},{1,5},{5,9},{9,13},{2,6},{6,10},{10,14},{3,7},{... | collective-permute-start | bytes 49160 | tf_op jit(solution)/shard_map/ppermute | solution.py:14
  33.4 1.3 collective-permute-start.5
  34.7 1.6 collective-permute-start.9
  36.3 1.2 collective-permute-done.5
  37.5 3.5 %collective-permute-start.6 = (bf16[18,1,256]{2,1,0:T(2,128)(2,1)S(1)}, bf16[18,1,256]{2,1,0:T(2,128)(2,1)S(1)}, u32[]{:S(2)}, u32[]{:S(2)}) collective-permute-start(bf16[18,1,256]{2,1,0:T(2,128)(2,1)S(1)} %get-tuple-element.41), channel_id=1, source_target_pairs={{0,1},{1,2},{2,3},{4,5},{5,6},{6,7},{8,9},{9,10},{10,11},{12,13},{... | collective-permute-start | bytes 27656 | tf_op jit(solution)/shard_map/ppermute | solution.py:14
  40.9 1.3 collective-permute-start.7
  42.5 4.1 %collective-permute-done.7 = bf16[18,1,256]{2,1,0:T(2,128)(2,1)S(1)} collective-permute-done((bf16[18,1,256]{2,1,0:T(2,128)(2,1)S(1)}, bf16[18,1,256]{2,1,0:T(2,128)(2,1)S(1)}, u32[]{:S(2)}, u32[]{:S(2)}) %collective-permute-start.7) | collective-permute-done | bytes 9248 | tf_op jit(solution)/shard_map/ppermute | solution.py:15
  49.4 3.2 %collective-permute-start.10 = (bf16[1,32,256]{2,1,0:T(8,128)(2,1)S(1)}, bf16[1,32,256]{2,1,0:T(8,128)(2,1)S(1)}, u32[]{:S(2)}, u32[]{:S(2)}) collective-permute-start(bf16[1,32,256]{2,1,0:T(8,128)(2,1)S(1)} %get-tuple-element.45), channel_id=1, source_target_pairs={{0,4},{4,8},{8,12},{1,5},{5,9},{9,13},{2,6},{6,10},{10,14},{3,7},{... | collective-permute-start | bytes 49160 | tf_op jit(solution)/shard_map/ppermute | solution.py:14
  52.6 1.3 collective-permute-start.11
  56.5 1.3 collective-permute-start.12
  57.8 4.7 %collective-permute-start.13 = (bf16[18,1,256]{2,1,0:T(2,128)(2,1)S(1)}, bf16[18,1,256]{2,1,0:T(2,128)(2,1)S(1)}, u32[]{:S(2)}, u32[]{:S(2)}) collective-permute-start(bf16[18,1,256]{2,1,0:T(2,128)(2,1)S(1)} %get-tuple-element.38), channel_id=1, source_target_pairs={{0,1},{1,2},{2,3},{4,5},{5,6},{6,7},{8,9},{9,10},{10,11},{12,13},{... | collective-permute-start | bytes 27656 | tf_op jit(solution)/shard_map/ppermute | solution.py:14
  62.9 0.9 collective-permute-done.13
  72.5 1.4 collective-permute-start.8
  73.9 7.5 %collective-permute-done.8 = bf16[16,32,256]{2,1,0:T(8,128)(2,1)S(1)} collective-permute-done((bf16[16,32,256]{2,1,0:T(8,128)(2,1)S(1)}, bf16[16,32,256]{2,1,0:T(8,128)(2,1)S(1)}, u32[]{:S(2)}, u32[]{:S(2)}) %collective-permute-start.8) | collective-permute-done | bytes 262176 | tf_op jit(solution)/shard_map/ppermute | solution.py:27
  81.3 132.7 %all-reduce.3.cloned.1.call-done = (f32[3,3,128,128]{3,2,1,0:T(8,128)}, f32[128,256]{1,0:T(8,128)}, f32[3,3,256,256]{3,2,1,0:T(8,128)}) async-done(((f32[3,3,128,128]{3,2,1,0:T(8,128)}, f32[128,256]{1,0:T(8,128)}, f32[3,3,256,256]{3,2,1,0:T(8,128)}), (f32[3,3,128,128]{3,2,1,0:T(8,128)}, f32[128,256]{1,0:T(8,128)}, f32[3,3,256,256]{3,2,1,0:T(8,128)})) %all-reduce.3.cloned.1.call-update) | async-done | bytes 3080208 | tf_op jit(solution)/shard_map/psum | solution.py:139
  214.8 1.9 copy.32
  217.3 3.2 %copy.34 = f32[3,3,256,256]{3,2,1,0:T(8,128)} copy(f32[3,3,256,256]{3,2,1,0:T(8,128)} %get-tuple-element.63) | data formatting | bytes 4718592
  (96 shorter events, 22.2 us)
Async XLA Ops:
  7.2 23.0 %copy-start = (bf16[128,256]{1,0:T(8,128)(2,1)S(1)}, bf16[128,256]{1,0:T(8,128)(2,1)}, u32[]{:S(2)}) copy-start(bf16[128,256]{1,0:T(8,128)(2,1)} %param.7) | copy-start | bytes 196612
  7.2 15.6 %copy-start.5 = (bf16[3,3,128,128]{3,2,1,0:T(8,128)(2,1)S(1)}, bf16[3,3,128,128]{3,2,1,0:T(8,128)(2,1)}, u32[]{:S(2)}) copy-start(bf16[3,3,128,128]{3,2,1,0:T(8,128)(2,1)} %param.6) | copy-start | bytes 884740
  7.2 206.9 %all-reduce.3.cloned.1.call-start = ((), (), s32[]{:S(2)}) async-start(), calls=%async_computation | async-start | bytes 6160384 | tf_op jit(solution)/shard_map/psum | solution.py:139
  8.0 3.7 %collective-permute-start = (bf16[1,64,128]{2,1,0:T(8,128)(2,1)S(1)}, bf16[1,64,128]{2,1,0:T(8,128)(2,1)S(1)}, u32[]{:S(2)}, u32[]{:S(2)}) collective-permute-start(bf16[1,64,128]{2,1,0:T(8,128)(2,1)S(1)} %get-tuple-element.21), channel_id=1, source_target_pairs={{0,4},{4,8},{8,12},{1,5},{5,9},{9,13},{2,6},{6,10},{10,14},{3,7},{... | collective-permute-start | bytes 49160 | tf_op jit(solution)/shard_map/ppermute | solution.py:14
  10.4 5.2 %collective-permute-start.1 = (bf16[1,64,128]{2,1,0:T(8,128)(2,1)S(1)}, bf16[1,64,128]{2,1,0:T(8,128)(2,1)S(1)}, u32[]{:S(2)}, u32[]{:S(2)}) collective-permute-start(bf16[1,64,128]{2,1,0:T(8,128)(2,1)S(1)} %get-tuple-element.22), channel_id=1, source_target_pairs={{4,0},{8,4},{12,8},{5,1},{9,5},{13,9},{6,2},{10,6},{14,10},{7,3},{... | collective-permute-start | bytes 49160 | tf_op jit(solution)/shard_map/ppermute | solution.py:15
  16.5 6.5 %collective-permute-start.2 = (bf16[34,1,128]{2,1,0:T(2,128)(2,1)S(1)}, bf16[34,1,128]{2,1,0:T(2,128)(2,1)S(1)}, u32[]{:S(2)}, u32[]{:S(2)}) collective-permute-start(bf16[34,1,128]{2,1,0:T(2,128)(2,1)S(1)} %get-tuple-element.15), channel_id=1, source_target_pairs={{0,1},{1,2},{2,3},{4,5},{5,6},{6,7},{8,9},{9,10},{10,11},{12,13},{... | collective-permute-start | bytes 26120 | tf_op jit(solution)/shard_map/ppermute | solution.py:14
  20.0 5.8 %copy-start.1 = (bf16[1,32,64,128]{3,2,1,0:T(8,128)(2,1)S(1)}, bf16[1,32,64,128]{3,2,1,0:T(8,128)(2,1)}, u32[]{:S(2)}) copy-start(bf16[1,32,64,128]{3,2,1,0:T(8,128)(2,1)} %param.5) | copy-start | bytes 1572868
  20.0 5.8 %collective-permute-start.3 = (bf16[34,1,128]{2,1,0:T(2,128)(2,1)S(1)}, bf16[34,1,128]{2,1,0:T(2,128)(2,1)S(1)}, u32[]{:S(2)}, u32[]{:S(2)}) collective-permute-start(bf16[34,1,128]{2,1,0:T(2,128)(2,1)S(1)} %get-tuple-element.16), channel_id=1, source_target_pairs={{1,0},{2,1},{3,2},{5,4},{6,5},{7,6},{9,8},{10,9},{11,10},{13,12},{... | collective-permute-start | bytes 26120 | tf_op jit(solution)/shard_map/ppermute | solution.py:15
  29.2 5.4 %copy-start.7 = (bf16[1,16,32,256]{3,2,1,0:T(8,128)(2,1)S(1)}, bf16[1,16,32,256]{3,2,1,0:T(8,128)(2,1)}, u32[]{:S(2)}) copy-start(bf16[1,16,32,256]{3,2,1,0:T(8,128)(2,1)} %param.9) | copy-start | bytes 786436
  29.3 13.0 %copy-start.2 = (bf16[3,3,256,256]{3,2,1,0:T(8,128)(2,1)S(1)}, bf16[3,3,256,256]{3,2,1,0:T(8,128)(2,1)}, u32[]{:S(2)}) copy-start(bf16[3,3,256,256]{3,2,1,0:T(8,128)(2,1)} %param.8) | copy-start | bytes 3538948
  30.4 5.9 %collective-permute-start.4 = (bf16[1,32,256]{2,1,0:T(8,128)(2,1)S(1)}, bf16[1,32,256]{2,1,0:T(8,128)(2,1)S(1)}, u32[]{:S(2)}, u32[]{:S(2)}) collective-permute-start(bf16[1,32,256]{2,1,0:T(8,128)(2,1)S(1)} %get-tuple-element.49), channel_id=1, source_target_pairs={{0,4},{4,8},{8,12},{1,5},{5,9},{9,13},{2,6},{6,10},{10,14},{3,7},{... | collective-permute-start | bytes 49160 | tf_op jit(solution)/shard_map/ppermute | solution.py:14
  33.4 4.0 %collective-permute-start.5 = (bf16[1,32,256]{2,1,0:T(8,128)(2,1)S(1)}, bf16[1,32,256]{2,1,0:T(8,128)(2,1)S(1)}, u32[]{:S(2)}, u32[]{:S(2)}) collective-permute-start(bf16[1,32,256]{2,1,0:T(8,128)(2,1)S(1)} %get-tuple-element.50), channel_id=1, source_target_pairs={{4,0},{8,4},{12,8},{5,1},{9,5},{13,9},{6,2},{10,6},{14,10},{7,3},{... | collective-permute-start | bytes 49160 | tf_op jit(solution)/shard_map/ppermute | solution.py:15
  34.7 14.0 %collective-permute-start.9 = (bf16[16,32,256]{2,1,0:T(8,128)(2,1)S(1)}, bf16[16,32,256]{2,1,0:T(8,128)(2,1)S(1)}, u32[]{:S(2)}, u32[]{:S(2)}) collective-permute-start(bf16[16,32,256]{2,1,0:T(8,128)(2,1)S(1)} %bitcast.331), channel_id=1, source_target_pairs={{0,16},{16,0},{1,17},{17,1},{2,18},{18,2},{3,19},{19,3},{4,20},{20... | collective-permute-start | bytes 786440 | tf_op jit(solution)/shard_map/ppermute | solution.py:27
  37.5 5.1 %collective-permute-start.6 = (bf16[18,1,256]{2,1,0:T(2,128)(2,1)S(1)}, bf16[18,1,256]{2,1,0:T(2,128)(2,1)S(1)}, u32[]{:S(2)}, u32[]{:S(2)}) collective-permute-start(bf16[18,1,256]{2,1,0:T(2,128)(2,1)S(1)} %get-tuple-element.41), channel_id=1, source_target_pairs={{0,1},{1,2},{2,3},{4,5},{5,6},{6,7},{8,9},{9,10},{10,11},{12,13},{... | collective-permute-start | bytes 27656 | tf_op jit(solution)/shard_map/ppermute | solution.py:14
  40.9 5.7 %collective-permute-start.7 = (bf16[18,1,256]{2,1,0:T(2,128)(2,1)S(1)}, bf16[18,1,256]{2,1,0:T(2,128)(2,1)S(1)}, u32[]{:S(2)}, u32[]{:S(2)}) collective-permute-start(bf16[18,1,256]{2,1,0:T(2,128)(2,1)S(1)} %get-tuple-element.42), channel_id=1, source_target_pairs={{1,0},{2,1},{3,2},{5,4},{6,5},{7,6},{9,8},{10,9},{11,10},{13,12},{... | collective-permute-start | bytes 27656 | tf_op jit(solution)/shard_map/ppermute | solution.py:15
  49.4 6.8 %collective-permute-start.10 = (bf16[1,32,256]{2,1,0:T(8,128)(2,1)S(1)}, bf16[1,32,256]{2,1,0:T(8,128)(2,1)S(1)}, u32[]{:S(2)}, u32[]{:S(2)}) collective-permute-start(bf16[1,32,256]{2,1,0:T(8,128)(2,1)S(1)} %get-tuple-element.45), channel_id=1, source_target_pairs={{0,4},{4,8},{8,12},{1,5},{5,9},{9,13},{2,6},{6,10},{10,14},{3,7},{... | collective-permute-start | bytes 49160 | tf_op jit(solution)/shard_map/ppermute | solution.py:14
  52.6 3.9 %collective-permute-start.11 = (bf16[1,32,256]{2,1,0:T(8,128)(2,1)S(1)}, bf16[1,32,256]{2,1,0:T(8,128)(2,1)S(1)}, u32[]{:S(2)}, u32[]{:S(2)}) collective-permute-start(bf16[1,32,256]{2,1,0:T(8,128)(2,1)S(1)} %get-tuple-element.46), channel_id=1, source_target_pairs={{4,0},{8,4},{12,8},{5,1},{9,5},{13,9},{6,2},{10,6},{14,10},{7,3},{... | collective-permute-start | bytes 49160 | tf_op jit(solution)/shard_map/ppermute | solution.py:15
  56.1 7.9 %copy-start.3 = (f32[9,256,256]{2,1,0:T(8,128)}, f32[9,256,256]{2,1,0:T(8,128)S(1)}, u32[]{:S(2)}) copy-start(f32[9,256,256]{2,1,0:T(8,128)S(1)} %fusion.4) | copy-start | bytes 7077892
  56.5 6.3 %collective-permute-start.12 = (bf16[18,1,256]{2,1,0:T(2,128)(2,1)S(1)}, bf16[18,1,256]{2,1,0:T(2,128)(2,1)S(1)}, u32[]{:S(2)}, u32[]{:S(2)}) collective-permute-start(bf16[18,1,256]{2,1,0:T(2,128)(2,1)S(1)} %get-tuple-element.37), channel_id=1, source_target_pairs={{1,0},{2,1},{3,2},{5,4},{6,5},{7,6},{9,8},{10,9},{11,10},{13,12},{... | collective-permute-start | bytes 27656 | tf_op jit(solution)/shard_map/ppermute | solution.py:15
  57.8 6.0 %collective-permute-start.13 = (bf16[18,1,256]{2,1,0:T(2,128)(2,1)S(1)}, bf16[18,1,256]{2,1,0:T(2,128)(2,1)S(1)}, u32[]{:S(2)}, u32[]{:S(2)}) collective-permute-start(bf16[18,1,256]{2,1,0:T(2,128)(2,1)S(1)} %get-tuple-element.38), channel_id=1, source_target_pairs={{0,1},{1,2},{2,3},{4,5},{5,6},{6,7},{8,9},{9,10},{10,11},{12,13},{... | collective-permute-start | bytes 27656 | tf_op jit(solution)/shard_map/ppermute | solution.py:14
  71.6 0.8 copy-start.4
  72.5 8.9 %collective-permute-start.8 = (bf16[16,32,256]{2,1,0:T(8,128)(2,1)S(1)}, bf16[16,32,256]{2,1,0:T(8,128)(2,1)S(1)}, u32[]{:S(2)}, u32[]{:S(2)}) collective-permute-start(bf16[16,32,256]{2,1,0:T(8,128)(2,1)S(1)} %bitcast.332), channel_id=1, source_target_pairs={{0,16},{16,0},{1,17},{17,1},{2,18},{18,2},{3,19},{19,3},{4,20},{20... | collective-permute-start | bytes 786440 | tf_op jit(solution)/shard_map/ppermute | solution.py:27
  214.0 2.6 %copy-start.6 = (f32[128,256]{1,0:T(8,128)S(1)}, f32[128,256]{1,0:T(8,128)}, u32[]{:S(2)}) copy-start(f32[128,256]{1,0:T(8,128)} %get-tuple-element.62) | copy-start | bytes 393220
Sparse Core Ops, SparseCore 0:
  72.6 141.4 all-reduce.2
where the time goes:
time: 228 us; the launch traced here: 227 us
  waiting for transfers between devices  153 us (67%)
  starting transfers between devices  31.2 us (14%)
  between operations  14.7 us (6%)
  matrix products  14.2 us (6%)
  local copies, waits for them, and re-layouts  9.64 us (4%)
  other arithmetic  4.38 us (2%)
    psum x1, waiting for transfers between devices, per_device(): lax.psum((grad_first, grad_projection, grad_second), ('section', 'gy', 'g...  133 us
    ppermute x6, starting transfers between devices, padded_2(): before = lax.ppermute(last, axis, up)  20.3 us
    ppermute x6, waiting for transfers between devices, padded_2(): after = lax.ppermute(initial, axis, down)  12.2 us
    ppermute x6, starting transfers between devices, padded_2(): after = lax.ppermute(initial, axis, down)  7.88 us
    ppermute x2, waiting for transfers between devices, from_partner(): return lax.ppermute(block, axis, route)  7.47 us
    unnamed x20, local copies, waits for them, and re-layouts  7.35 us
    dot_general x18, matrix products, conv_slopes(): jnp.einsum('pc,pd->cd', piece, slope, preferred_element_type=jnp.float32)  5.6 us
    dot_general x18, matrix products, conv_forward(): jnp.dot(piece, kernel[row_tap, col_tap], preferred_element_type=jnp.float32)  4.91 us
  transfers between devices with their start and end apart: 15, of which 8 were waited for; matrix products, arithmetic and copies ran while one was open for 3% of the time, Pallas kernels for 0%

commit v1 on v0

--- a/solution.py
+++ b/solution.py
@@ -2,6 +2,9 @@
 import jax.numpy as jnp
 from jax import lax
 from jax.sharding import PartitionSpec as P
+
+
+GY = ("gy_hi", "core")
 
 
 def padded_2(array, sides, width):
@@ -71,7 +74,7 @@
 
 def first_forward(tile, first_kernel):
     row_count, col_count, channels = tile.shape
-    padded = padded_2(tile, (("gy", 0), ("gx", 1)), 1)
+    padded = padded_2(tile, ((GY, 0), ("gx", 1)), 1)
     before = conv_forward(padded, first_kernel, row_count, col_count)
     hidden = jax.nn.silu(before).astype(jnp.bfloat16).reshape(row_count, col_count, channels)
     pooled = (
@@ -95,13 +98,13 @@
 
 def second_pass(middle, second_kernel, upstream):
     half_rows, half_cols, wide = middle.shape
-    padded = padded_2(middle, (("gy", 0), ("gx", 1)), 1)
+    padded = padded_2(middle, ((GY, 0), ("gx", 1)), 1)
     before = conv_forward(padded, second_kernel, half_rows, half_cols)
     output = jax.nn.silu(before).astype(jnp.bfloat16).reshape(half_rows, half_cols, wide)
     flat_up = upstream.reshape(half_rows * half_cols, wide).astype(jnp.float32)
     slope = (flat_up * silu_slope(before)).astype(jnp.bfloat16)
     kernel_grad = conv_slopes(padded, slope, half_rows, half_cols)
-    slope_padded = padded_2(slope.reshape(half_rows, half_cols, wide), (("gy", 0), ("gx", 1)), 1)
+    slope_padded = padded_2(slope.reshape(half_rows, half_cols, wide), ((GY, 0), ("gx", 1)), 1)
     back = conv_back(slope_padded, second_kernel, half_rows, half_cols).astype(jnp.bfloat16)
     return (output, kernel_grad, back.reshape(half_rows, half_cols, wide))
 
@@ -126,6 +129,55 @@
     spread = spread.reshape(4 * half_rows * half_cols, channels)
     slope = (spread * silu_slope(before)).astype(jnp.bfloat16)
     return conv_slopes(padded, slope, 2 * half_rows, 2 * half_cols)
+
+
+def swap_pairs(block, axis):
+    return lax.ppermute(block, axis, [(0, 1), (1, 0)])
+
+
+def reduce_all(first, proj, second):
+    plane, line = ("section", "gy_hi"), "gx"
+    planes = lax.axis_size("section") * lax.axis_size("gy_hi")
+    lines = lax.axis_size(line)
+    wide = proj.shape[1]
+    flat_first = first.reshape(-1, first.shape[3])
+    fold = wide // first.shape[3]
+    seg = flat_first.shape[0] // fold
+    folded = jnp.concatenate([flat_first[i * seg : (i + 1) * seg] for i in range(fold)], axis=1)
+    flat_second = second.reshape(-1, wide)
+    rows = [folded.shape[0], proj.shape[0], flat_second.shape[0]]
+    total = sum(rows)
+    unit = 2 * planes * lines * 16
+    padded = -(-total // unit) * unit
+    flat = jnp.concatenate(
+        [flat_second, proj, folded, jnp.zeros((padded - total, wide), jnp.float32)], axis=0
+    )
+    half = padded // 2
+    core = lax.axis_index("core")
+    low, high = flat[:half], flat[half:]
+    mine = jnp.where(core == 0, low, high)
+    other = jnp.where(core == 0, high, low).astype(jnp.bfloat16)
+    summed = mine + swap_pairs(other, "core").astype(jnp.float32)
+    for axes, count in ((plane, planes), (line, lines)):
+        parts = summed.astype(jnp.bfloat16).reshape(count, summed.shape[0] // count, wide)
+        parts = lax.all_to_all(parts, axes, 0, 0, tiled=True)
+        summed = parts.astype(jnp.float32).sum(axis=0)
+    whole = summed.astype(jnp.bfloat16)
+    for axes, count in ((line, lines), (plane, planes)):
+        parts = jnp.broadcast_to(whole[None], (count,) + whole.shape)
+        whole = lax.all_to_all(parts, axes, 0, 0, tiled=True).reshape(-1, wide)
+    theirs = swap_pairs(whole, "core")
+    low = jnp.where(core == 0, whole, theirs)
+    high = jnp.where(core == 0, theirs, whole)
+    flat = jnp.concatenate([low, high], axis=0).astype(jnp.float32)
+    second = flat[: rows[2]].reshape(second.shape)
+    proj = flat[rows[2] : rows[2] + rows[1]]
+    folded = flat[rows[2] + rows[1] : total]
+    width = first.shape[3]
+    first = jnp.concatenate(
+        [folded[:, i * width : (i + 1) * width] for i in range(fold)], axis=0
+    ).reshape(first.shape)
+    return first, proj, second
 
 
 def per_device(images, first_kernel, projection, second_kernel, cotangent):
@@ -136,18 +188,21 @@
     grad_projection, pooled_slope = projection_back(pooled, back, projection)
     output = from_partner(output, "section", 0)
     grad_first = first_back(padded, before, pooled_slope)
-    grad_first, grad_projection, grad_second = lax.psum(
-        (grad_first, grad_projection, grad_second), ("section", "gy", "gx")
+    grad_first, grad_projection, grad_second = reduce_all(
+        grad_first, grad_projection, grad_second
     )
     return (output[None], grad_first, grad_projection, grad_second)
 
 
 def solution(mesh):
-    placed = (P("section", "gy", "gx", None), P(), P(), P(), P("section", "gy", "gx", None))
+    shape = dict(mesh.shape)
+    grid = mesh.devices.reshape(shape["section"], shape["gy"] // 2, 2, shape["gx"])
+    split = jax.sharding.Mesh(grid, ("section", "gy_hi", "core", "gx"))
+    tiles = P("section", ("gy_hi", "core"), "gx", None)
     return jax.shard_map(
         per_device,
-        mesh=mesh,
-        in_specs=placed,
-        out_specs=(P("section", "gy", "gx", None), P(), P(), P()),
+        mesh=split,
+        in_specs=(tiles, P(), P(), P(), tiles),
+        out_specs=(tiles, P(), P(), P()),
         check_vma=False,
     )

time: 228 us -> 136 us (0.60)
  waiting for transfers between devices: 153 us -> 20.9 us
  blocking collectives: 0 us -> 48.1 us
  between operations: 14.7 us -> 1.35 us
  other arithmetic: 4.38 us -> 8.58 us
  local copies, waits for them, and re-layouts: 9.64 us -> 6.63 us
  matrix products: 14.2 us -> 16.9 us
    psum x1 -> x0, waiting for transfers between devices: 133 us -> none  [per_device(): lax.psum((grad_first, grad_projection, grad_second), ('section', 'gy', 'g...]
    all_to_all x0 -> x4, blocking collectives: none -> 48.1 us  [the longest x2 26.9 us: reduce_all(): parts = lax.all_to_all(parts, axes, 0, 0, tiled=True)]
    dot_general x18, matrix products: 4.91 us -> 8.42 us  [conv_forward(): jnp.dot(piece, kernel[row_tap, col_tap], preferred_element_type=jnp.float32)]
    unnamed x20 -> x29, local copies, waits for them, and re-layouts: 7.35 us -> 4.27 us
  transfers between devices with their start and end apart: 15 -> 16, of which waited for: 8 -> 8; matrix products, arithmetic and copies ran while one was open for 3% -> 10% of each run, Pallas kernels for 0% -> 0%
where the time goes in v1:
time: 136 us; the launch traced here: 135 us
  blocking collectives  48.1 us (35%)
  starting transfers between devices  33 us (24%)
  waiting for transfers between devices  20.9 us (15%)
  matrix products  16.9 us (12%)
  other arithmetic  8.58 us (6%)
  local copies, waits for them, and re-layouts  6.63 us (5%)
    all_to_all x2, blocking collectives, reduce_all(): parts = lax.all_to_all(parts, axes, 0, 0, tiled=True)  26.9 us
    all_to_all x2, blocking collectives, reduce_all(): whole = lax.all_to_all(parts, axes, 0, 0, tiled=True).reshape(-1, wide)  21.2 us
    ppermute x6, starting transfers between devices, padded_2(): before = lax.ppermute(last, axis, up)  20.4 us
    ppermute x6, waiting for transfers between devices, padded_2(): after = lax.ppermute(initial, axis, down)  10.2 us
    dot_general x18, matrix products, conv_forward(): jnp.dot(piece, kernel[row_tap, col_tap], preferred_element_type=jnp.float32)  8.42 us
    ppermute x6, starting transfers between devices, padded_2(): after = lax.ppermute(initial, axis, down)  7.88 us
    ppermute x2, waiting for transfers between devices, from_partner(): return lax.ppermute(block, axis, route)  7.81 us
    dot_general x18, matrix products, conv_slopes(): jnp.einsum('pc,pd->cd', piece, slope, preferred_element_type=jnp.float32)  5.48 us
  transfers between devices with their start and end apart: 16, of which 8 were waited for; matrix products, arithmetic and copies ran while one was open for 10% of the time, Pallas kernels for 0%

profile of v1, /device:TPU:0, one launch (start us, length us, event | category | flops | bytes accessed | tf_op | source)
XLA Modules:
  0.0 135.4 jit_solution(6191932572515208348)
XLA Ops:
  1.4 2.4 %collective-permute-start = (bf16[1,64,128]{2,1,0:T(8,128)(2,1)S(1)}, bf16[1,64,128]{2,1,0:T(8,128)(2,1)S(1)}, u32[]{:S(2)}, u32[]{:S(2)}) collective-permute-start(bf16[1,64,128]{2,1,0:T(8,128)(2,1)S(1)} %get-tuple-element.24), channel_id=1, source_target_pairs={{0,4},{4,8},{8,12},{1,5},{5,9},{9,13},{2,6},{6,10},{10,14},{3,7},{... | collective-permute-start | bytes 49160 | tf_op jit(solution)/shard_map/ppermute | solution.py:17
  5.1 2.4 %collective-permute-start.9 = (bf16[16,32,256]{2,1,0:T(8,128)(2,1)}, bf16[16,32,256]{2,1,0:T(8,128)(2,1)}, u32[]{:S(2)}, u32[]{:S(2)}) collective-permute-start(bf16[16,32,256]{2,1,0:T(8,128)(2,1)} %bitcast.343), channel_id=1, source_target_pairs={{0,16},{16,0},{1,17},{17,1},{2,18},{18,2},{3,19},{19,3},{4,20},{20... | collective-permute-start | bytes 786440 | tf_op jit(solution)/shard_map/ppermute | solution.py:30
  7.5 1.5 %collective-permute-done.1 = bf16[1,64,128]{2,1,0:T(8,128)(2,1)S(1)} collective-permute-done((bf16[1,64,128]{2,1,0:T(8,128)(2,1)S(1)}, bf16[1,64,128]{2,1,0:T(8,128)(2,1)S(1)}, u32[]{:S(2)}, u32[]{:S(2)}) %collective-permute-start.1) | collective-permute-done | bytes 16416 | tf_op jit(solution)/shard_map/ppermute | solution.py:18
  9.9 3.5 %collective-permute-start.2 = (bf16[34,1,128]{2,1,0:T(2,128)(2,1)S(1)}, bf16[34,1,128]{2,1,0:T(2,128)(2,1)S(1)}, u32[]{:S(2)}, u32[]{:S(2)}) collective-permute-start(bf16[34,1,128]{2,1,0:T(2,128)(2,1)S(1)} %get-tuple-element.18), channel_id=1, source_target_pairs={{0,1},{1,2},{2,3},{4,5},{5,6},{6,7},{8,9},{9,10},{10,11},{12,13},{... | collective-permute-start | bytes 26120 | tf_op jit(solution)/shard_map/ppermute | solution.py:17
  13.4 1.4 %collective-permute-start.3 = (bf16[34,1,128]{2,1,0:T(2,128)(2,1)S(1)}, bf16[34,1,128]{2,1,0:T(2,128)(2,1)S(1)}, u32[]{:S(2)}, u32[]{:S(2)}) collective-permute-start(bf16[34,1,128]{2,1,0:T(2,128)(2,1)S(1)} %get-tuple-element.19), channel_id=1, source_target_pairs={{1,0},{2,1},{3,2},{5,4},{6,5},{7,6},{9,8},{10,9},{11,10},{13,12},{... | collective-permute-start | bytes 26120 | tf_op jit(solution)/shard_map/ppermute | solution.py:18
  14.9 1.4 %pad_maximum_fusion.5 = (bf16[32,64,128]{2,1,0:T(8,128)(2,1)S(1)}, bf16[32,64,128]{2,1,0:T(8,128)(2,1)S(1)}) fusion(bf16[1,64,128]{2,1,0:T(8,128)(2,1)S(1)} %collective-permute-done.1, bf16[32,64,128]{2,1,0:T(8,128)(2,1)} %bitcast.281, bf16[1,64,128]{2,1,0:T(8,128)(2,1)S(1)} %collective-permute-done), kind=kLoop, calls=%fused_computation.79 | loop fusion | flops 524288 | bytes 1605632 | tf_op jit(solution)/shard_map/concatenate | solution.py:19
  16.6 2.6 %collective-permute-done.3 = bf16[34,1,128]{2,1,0:T(2,128)(2,1)S(1)} collective-permute-done((bf16[34,1,128]{2,1,0:T(2,128)(2,1)S(1)}, bf16[34,1,128]{2,1,0:T(2,128)(2,1)S(1)}, u32[]{:S(2)}, u32[]{:S(2)}) %collective-permute-start.3) | collective-permute-done | bytes 8736 | tf_op jit(solution)/shard_map/ppermute | solution.py:18
  22.5 1.4 %multiply_convert_fusion.1 = (bf16[2048,128]{1,0:T(8,128)(2,1)S(1)}, f32[2048,128]{1,0:T(8,128)}) fusion(f32[2048,128]{1,0:T(8,128)S(1)} %fusion.65, f32[2048,128]{1,0:T(8,128)S(1)} %convolution_add_fusion.1, bf16[2048,128]{1,0:T(8,128)(2,1)S(1)} %bitcast.322, bf16[3,3,128,128]{3,2,1,0:T(8,128)(2,1)S(1)} %copy-done.12), kind=kOutput, calls=%fused_computation.72 | convolution fusion | flops 68943872 | bytes 4227072 | tf_op jit(solution)/shard_map/dot_general | solution.py:45
  25.7 3.3 %collective-permute-start.4 = (bf16[1,32,256]{2,1,0:T(8,128)(2,1)S(1)}, bf16[1,32,256]{2,1,0:T(8,128)(2,1)S(1)}, u32[]{:S(2)}, u32[]{:S(2)}) collective-permute-start(bf16[1,32,256]{2,1,0:T(8,128)(2,1)S(1)} %get-tuple-element.64), channel_id=1, source_target_pairs={{0,4},{4,8},{8,12},{1,5},{5,9},{9,13},{2,6},{6,10},{10,14},{3,7},{... | collective-permute-start | bytes 49160 | tf_op jit(solution)/shard_map/ppermute | solution.py:17
  30.5 2.4 %collective-permute-done.5 = bf16[1,32,256]{2,1,0:T(8,128)(2,1)S(1)} collective-permute-done((bf16[1,32,256]{2,1,0:T(8,128)(2,1)S(1)}, bf16[1,32,256]{2,1,0:T(8,128)(2,1)S(1)}, u32[]{:S(2)}, u32[]{:S(2)}) %collective-permute-start.5) | collective-permute-done | bytes 16416 | tf_op jit(solution)/shard_map/ppermute | solution.py:18
  32.9 3.5 %collective-permute-start.6 = (bf16[18,1,256]{2,1,0:T(2,128)(2,1)S(1)}, bf16[18,1,256]{2,1,0:T(2,128)(2,1)S(1)}, u32[]{:S(2)}, u32[]{:S(2)}) collective-permute-start(bf16[18,1,256]{2,1,0:T(2,128)(2,1)S(1)} %get-tuple-element.44), channel_id=1, source_target_pairs={{0,1},{1,2},{2,3},{4,5},{5,6},{6,7},{8,9},{9,10},{10,11},{12,13},{... | collective-permute-start | bytes 27656 | tf_op jit(solution)/shard_map/ppermute | solution.py:17
  38.9 3.2 %collective-permute-done.7 = bf16[18,1,256]{2,1,0:T(2,128)(2,1)S(1)} collective-permute-done((bf16[18,1,256]{2,1,0:T(2,128)(2,1)S(1)}, bf16[18,1,256]{2,1,0:T(2,128)(2,1)S(1)}, u32[]{:S(2)}, u32[]{:S(2)}) %collective-permute-start.7) | collective-permute-done | bytes 9248 | tf_op jit(solution)/shard_map/ppermute | solution.py:18
  45.1 2.1 %fusion.24 = (bf16[512,256]{1,0:T(8,128)(2,1)S(1)}, bf16[512,256]{1,0:T(8,128)(2,1)}) fusion(bf16[16,32,256]{2,1,0:T(8,128)(2,1)} %collective-permute-done.9, f32[512,256]{1,0:T(8,128)S(1)} %fusion.27, f32[512,256]{1,0:T(8,128)S(1)} %convolution_add_fusion.15, bf16[512,256]{1,0:T(8,128)(2,1)S(1)} %bitcast.326, bf16[3,3,256,256]{3,2,1,0:T(8,128)(2,1)S(1)} %copy-done.6), kind=kOutput, calls=%fused_computation.82 | convolution fusion | flops 68943872 | bytes 2228224 | tf_op jit(solution)/shard_map/dot_general | solution.py:45
  47.5 2.9 %collective-permute-start.10 = (bf16[1,32,256]{2,1,0:T(8,128)(2,1)S(1)}, bf16[1,32,256]{2,1,0:T(8,128)(2,1)S(1)}, u32[]{:S(2)}, u32[]{:S(2)}) collective-permute-start(bf16[1,32,256]{2,1,0:T(8,128)(2,1)S(1)} %get-tuple-element.60), channel_id=1, source_target_pairs={{0,4},{4,8},{8,12},{1,5},{5,9},{9,13},{2,6},{6,10},{10,14},{3,7},{... | collective-permute-start | bytes 49160 | tf_op jit(solution)/shard_map/ppermute | solution.py:17
  54.5 1.3 collective-permute-start.12
  55.8 4.7 %collective-permute-start.13 = (bf16[18,1,256]{2,1,0:T(2,128)(2,1)S(1)}, bf16[18,1,256]{2,1,0:T(2,128)(2,1)S(1)}, u32[]{:S(2)}, u32[]{:S(2)}) collective-permute-start(bf16[18,1,256]{2,1,0:T(2,128)(2,1)S(1)} %get-tuple-element.41), channel_id=1, source_target_pairs={{0,1},{1,2},{2,3},{4,5},{5,6},{6,7},{8,9},{9,10},{10,11},{12,13},{... | collective-permute-start | bytes 27656 | tf_op jit(solution)/shard_map/ppermute | solution.py:17
  70.6 1.4 %collective-permute-start.14 = (bf16[1536,256]{1,0:T(8,128)(2,1)S(1)}, bf16[1536,256]{1,0:T(8,128)(2,1)S(1)}, u32[]{:S(2)}, u32[]{:S(2)}) collective-permute-start(bf16[1536,256]{1,0:T(8,128)(2,1)S(1)} %fusion.5), channel_id=1, source_target_pairs={{0,4},{4,0},{1,5},{5,1},{2,6},{6,2},{3,7},{7,3},{8,12},{12,8},{9,1... | collective-permute-start | bytes 2359304 | tf_op jit(solution)/shard_map/ppermute | solution.py:135
  72.0 1.9 %collective-permute-done.14 = bf16[1536,256]{1,0:T(8,128)(2,1)S(1)} collective-permute-done((bf16[1536,256]{1,0:T(8,128)(2,1)S(1)}, bf16[1536,256]{1,0:T(8,128)(2,1)S(1)}, u32[]{:S(2)}, u32[]{:S(2)}) %collective-permute-start.14) | collective-permute-done | bytes 786464 | tf_op jit(solution)/shard_map/ppermute | solution.py:135
  74.3 15.8 %all_to_all.20 = bf16[4,384,256]{2,1,0:T(8,128)(2,1)S(1)} all-to-all(bf16[4,384,256]{2,1,0:T(8,128)(2,1)S(1)} %bitcast.305), channel_id=1, replica_groups=mesh['section'=2,'gy_hi'=2,'core'=2,'gx'=4] {'section','gy_hi'}, dimensions={0} | all-to-all | bytes 1572864 | tf_op jit(solution)/shard_map/all_to_all | solution.py:163
  90.2 11.2 %all_to_all.21 = bf16[4,96,256]{2,1,0:T(8,128)(2,1)S(1)} all-to-all(bf16[4,96,256]{2,1,0:T(8,128)(2,1)S(1)} %bitcast.337), channel_id=1, replica_groups=mesh['section'=2,'gy_hi'=2,'core'=2,'gx'=4] {'gx'}, dimensions={0} | all-to-all | bytes 393216 | tf_op jit(solution)/shard_map/all_to_all | solution.py:163
  101.4 9.3 %all_to_all.22 = bf16[4,96,256]{2,1,0:T(8,128)(2,1)S(1)} all-to-all(bf16[4,96,256]{2,1,0:T(8,128)(2,1)S(1)} %broadcast_in_dim.28), channel_id=1, replica_groups=mesh['section'=2,'gy_hi'=2,'core'=2,'gx'=4] {'gx'}, dimensions={0} | all-to-all | bytes 393216 | tf_op jit(solution)/shard_map/all_to_all | solution.py:168
  110.8 11.9 %all_to_all.23 = bf16[4,384,256]{2,1,0:T(8,128)(2,1)S(1)} all-to-all(bf16[4,384,256]{2,1,0:T(8,128)(2,1)S(1)} %broadcast_in_dim.30), channel_id=1, replica_groups=mesh['section'=2,'gy_hi'=2,'core'=2,'gx'=4] {'section','gy_hi'}, dimensions={0} | all-to-all | bytes 1572864 | tf_op jit(solution)/shard_map/all_to_all | solution.py:168
  123.6 7.8 %collective-permute-done.8 = bf16[16,32,256]{2,1,0:T(8,128)(2,1)S(1)} collective-permute-done((bf16[16,32,256]{2,1,0:T(8,128)(2,1)S(1)}, bf16[16,32,256]{2,1,0:T(8,128)(2,1)S(1)}, u32[]{:S(2)}, u32[]{:S(2)}) %collective-permute-start.8) | collective-permute-done | bytes 262176 | tf_op jit(solution)/shard_map/ppermute | solution.py:30
  132.2 1.6 %fusion.9 = f32[2304,256]{1,0:T(8,128)} fusion(bf16[1536,256]{1,0:T(8,128)(2,1)S(1)} %get-tuple-element.7, bf16[1536,256]{1,0:T(8,128)(2,1)S(1)} %get-tuple-element.6), kind=kLoop, calls=%fused_computation.36 | loop fusion | flops 2359296 | bytes 3932160 | tf_op jit(solution)/shard_map/convert_element_type | solution.py:172
  (124 shorter events, 33.2 us)
Async XLA Ops:
  0.6 24.8 %copy-start = (bf16[128,256]{1,0:T(8,128)(2,1)S(1)}, bf16[128,256]{1,0:T(8,128)(2,1)}, u32[]{:S(2)}) copy-start(bf16[128,256]{1,0:T(8,128)(2,1)} %param.7) | copy-start | bytes 196612
  0.6 15.7 %copy-start.12 = (bf16[3,3,128,128]{3,2,1,0:T(8,128)(2,1)S(1)}, bf16[3,3,128,128]{3,2,1,0:T(8,128)(2,1)}, u32[]{:S(2)}) copy-start(bf16[3,3,128,128]{3,2,1,0:T(8,128)(2,1)} %param.6) | copy-start | bytes 884740
  1.4 6.1 %collective-permute-start = (bf16[1,64,128]{2,1,0:T(8,128)(2,1)S(1)}, bf16[1,64,128]{2,1,0:T(8,128)(2,1)S(1)}, u32[]{:S(2)}, u32[]{:S(2)}) collective-permute-start(bf16[1,64,128]{2,1,0:T(8,128)(2,1)S(1)} %get-tuple-element.24), channel_id=1, source_target_pairs={{0,4},{4,8},{8,12},{1,5},{5,9},{9,13},{2,6},{6,10},{10,14},{3,7},{... | collective-permute-start | bytes 49160 | tf_op jit(solution)/shard_map/ppermute | solution.py:17
  3.8 5.2 %collective-permute-start.1 = (bf16[1,64,128]{2,1,0:T(8,128)(2,1)S(1)}, bf16[1,64,128]{2,1,0:T(8,128)(2,1)S(1)}, u32[]{:S(2)}, u32[]{:S(2)}) collective-permute-start(bf16[1,64,128]{2,1,0:T(8,128)(2,1)S(1)} %get-tuple-element.25), channel_id=1, source_target_pairs={{4,0},{8,4},{12,8},{5,1},{9,5},{13,9},{6,2},{10,6},{14,10},{7,3},{... | collective-permute-start | bytes 49160 | tf_op jit(solution)/shard_map/ppermute | solution.py:18
  5.1 40.0 %collective-permute-start.9 = (bf16[16,32,256]{2,1,0:T(8,128)(2,1)}, bf16[16,32,256]{2,1,0:T(8,128)(2,1)}, u32[]{:S(2)}, u32[]{:S(2)}) collective-permute-start(bf16[16,32,256]{2,1,0:T(8,128)(2,1)} %bitcast.343), channel_id=1, source_target_pairs={{0,16},{16,0},{1,17},{17,1},{2,18},{18,2},{3,19},{19,3},{4,20},{20... | collective-permute-start | bytes 786440 | tf_op jit(solution)/shard_map/ppermute | solution.py:30
  9.9 6.6 %collective-permute-start.2 = (bf16[34,1,128]{2,1,0:T(2,128)(2,1)S(1)}, bf16[34,1,128]{2,1,0:T(2,128)(2,1)S(1)}, u32[]{:S(2)}, u32[]{:S(2)}) collective-permute-start(bf16[34,1,128]{2,1,0:T(2,128)(2,1)S(1)} %get-tuple-element.18), channel_id=1, source_target_pairs={{0,1},{1,2},{2,3},{4,5},{5,6},{6,7},{8,9},{9,10},{10,11},{12,13},{... | collective-permute-start | bytes 26120 | tf_op jit(solution)/shard_map/ppermute | solution.py:17
  13.4 5.8 %copy-start.1 = (bf16[1,32,64,128]{3,2,1,0:T(8,128)(2,1)S(1)}, bf16[1,32,64,128]{3,2,1,0:T(8,128)(2,1)}, u32[]{:S(2)}) copy-start(bf16[1,32,64,128]{3,2,1,0:T(8,128)(2,1)} %param.5) | copy-start | bytes 1572868
  13.4 5.8 %collective-permute-start.3 = (bf16[34,1,128]{2,1,0:T(2,128)(2,1)S(1)}, bf16[34,1,128]{2,1,0:T(2,128)(2,1)S(1)}, u32[]{:S(2)}, u32[]{:S(2)}) collective-permute-start(bf16[34,1,128]{2,1,0:T(2,128)(2,1)S(1)} %get-tuple-element.19), channel_id=1, source_target_pairs={{1,0},{2,1},{3,2},{5,4},{6,5},{7,6},{9,8},{10,9},{11,10},{13,12},{... | collective-permute-start | bytes 26120 | tf_op jit(solution)/shard_map/ppermute | solution.py:18
  16.3 6.2 %copy-start.7 = (bf16[32,64,128]{2,1,0:T(8,128)(2,1)}, bf16[32,64,128]{2,1,0:T(8,128)(2,1)S(1)}, u32[]{:S(2)}) copy-start(bf16[32,64,128]{2,1,0:T(8,128)(2,1)S(1)} %get-tuple-element.22) | copy-start | bytes 1572868
  25.7 4.7 %collective-permute-start.4 = (bf16[1,32,256]{2,1,0:T(8,128)(2,1)S(1)}, bf16[1,32,256]{2,1,0:T(8,128)(2,1)S(1)}, u32[]{:S(2)}, u32[]{:S(2)}) collective-permute-start(bf16[1,32,256]{2,1,0:T(8,128)(2,1)S(1)} %get-tuple-element.64), channel_id=1, source_target_pairs={{0,4},{4,8},{8,12},{1,5},{5,9},{9,13},{2,6},{6,10},{10,14},{3,7},{... | collective-permute-start | bytes 49160 | tf_op jit(solution)/shard_map/ppermute | solution.py:17
  29.1 3.8 %collective-permute-start.5 = (bf16[1,32,256]{2,1,0:T(8,128)(2,1)S(1)}, bf16[1,32,256]{2,1,0:T(8,128)(2,1)S(1)}, u32[]{:S(2)}, u32[]{:S(2)}) collective-permute-start(bf16[1,32,256]{2,1,0:T(8,128)(2,1)S(1)} %get-tuple-element.65), channel_id=1, source_target_pairs={{4,0},{8,4},{12,8},{5,1},{9,5},{13,9},{6,2},{10,6},{14,10},{7,3},{... | collective-permute-start | bytes 49160 | tf_op jit(solution)/shard_map/ppermute | solution.py:18
  32.9 6.0 %collective-permute-start.6 = (bf16[18,1,256]{2,1,0:T(2,128)(2,1)S(1)}, bf16[18,1,256]{2,1,0:T(2,128)(2,1)S(1)}, u32[]{:S(2)}, u32[]{:S(2)}) collective-permute-start(bf16[18,1,256]{2,1,0:T(2,128)(2,1)S(1)} %get-tuple-element.44), channel_id=1, source_target_pairs={{0,1},{1,2},{2,3},{4,5},{5,6},{6,7},{8,9},{9,10},{10,11},{12,13},{... | collective-permute-start | bytes 27656 | tf_op jit(solution)/shard_map/ppermute | solution.py:17
  36.4 5.7 %collective-permute-start.7 = (bf16[18,1,256]{2,1,0:T(2,128)(2,1)S(1)}, bf16[18,1,256]{2,1,0:T(2,128)(2,1)S(1)}, u32[]{:S(2)}, u32[]{:S(2)}) collective-permute-start(bf16[18,1,256]{2,1,0:T(2,128)(2,1)S(1)} %get-tuple-element.45), channel_id=1, source_target_pairs={{1,0},{2,1},{3,2},{5,4},{6,5},{7,6},{9,8},{10,9},{11,10},{13,12},{... | collective-permute-start | bytes 27656 | tf_op jit(solution)/shard_map/ppermute | solution.py:18
  42.2 1.3 copy-start.6
  47.5 6.5 %collective-permute-start.10 = (bf16[1,32,256]{2,1,0:T(8,128)(2,1)S(1)}, bf16[1,32,256]{2,1,0:T(8,128)(2,1)S(1)}, u32[]{:S(2)}, u32[]{:S(2)}) collective-permute-start(bf16[1,32,256]{2,1,0:T(8,128)(2,1)S(1)} %get-tuple-element.60), channel_id=1, source_target_pairs={{0,4},{4,8},{8,12},{1,5},{5,9},{9,13},{2,6},{6,10},{10,14},{3,7},{... | collective-permute-start | bytes 49160 | tf_op jit(solution)/shard_map/ppermute | solution.py:17
  50.4 4.0 %collective-permute-start.11 = (bf16[1,32,256]{2,1,0:T(8,128)(2,1)S(1)}, bf16[1,32,256]{2,1,0:T(8,128)(2,1)S(1)}, u32[]{:S(2)}, u32[]{:S(2)}) collective-permute-start(bf16[1,32,256]{2,1,0:T(8,128)(2,1)S(1)} %get-tuple-element.61), channel_id=1, source_target_pairs={{4,0},{8,4},{12,8},{5,1},{9,5},{13,9},{6,2},{10,6},{14,10},{7,3},{... | collective-permute-start | bytes 49160 | tf_op jit(solution)/shard_map/ppermute | solution.py:18
  54.5 6.3 %collective-permute-start.12 = (bf16[18,1,256]{2,1,0:T(2,128)(2,1)S(1)}, bf16[18,1,256]{2,1,0:T(2,128)(2,1)S(1)}, u32[]{:S(2)}, u32[]{:S(2)}) collective-permute-start(bf16[18,1,256]{2,1,0:T(2,128)(2,1)S(1)} %get-tuple-element.40), channel_id=1, source_target_pairs={{1,0},{2,1},{3,2},{5,4},{6,5},{7,6},{9,8},{10,9},{11,10},{13,12},{... | collective-permute-start | bytes 27656 | tf_op jit(solution)/shard_map/ppermute | solution.py:18
  55.8 6.0 %collective-permute-start.13 = (bf16[18,1,256]{2,1,0:T(2,128)(2,1)S(1)}, bf16[18,1,256]{2,1,0:T(2,128)(2,1)S(1)}, u32[]{:S(2)}, u32[]{:S(2)}) collective-permute-start(bf16[18,1,256]{2,1,0:T(2,128)(2,1)S(1)} %get-tuple-element.41), channel_id=1, source_target_pairs={{0,1},{1,2},{2,3},{4,5},{5,6},{6,7},{8,9},{9,10},{10,11},{12,13},{... | collective-permute-start | bytes 27656 | tf_op jit(solution)/shard_map/ppermute | solution.py:17
  64.8 1.2 copy-start.11
  65.7 1.1 copy-start.5
  70.6 3.3 %collective-permute-start.14 = (bf16[1536,256]{1,0:T(8,128)(2,1)S(1)}, bf16[1536,256]{1,0:T(8,128)(2,1)S(1)}, u32[]{:S(2)}, u32[]{:S(2)}) collective-permute-start(bf16[1536,256]{1,0:T(8,128)(2,1)S(1)} %fusion.5), channel_id=1, source_target_pairs={{0,4},{4,0},{1,5},{5,1},{2,6},{6,2},{3,7},{7,3},{8,12},{12,8},{9,1... | collective-permute-start | bytes 2359304 | tf_op jit(solution)/shard_map/ppermute | solution.py:135
  101.4 21.3 %copy-start.13 = (bf16[512,256]{1,0:T(8,128)(2,1)S(1)}, bf16[512,256]{1,0:T(8,128)(2,1)}, u32[]{:S(2)}) copy-start(bf16[512,256]{1,0:T(8,128)(2,1)} %get-tuple-element.21) | copy-start | bytes 786436
  122.7 8.7 %collective-permute-start.15 = (bf16[1536,256]{1,0:T(8,128)(2,1)S(1)}, bf16[1536,256]{1,0:T(8,128)(2,1)S(1)}, u32[]{:S(2)}, u32[]{:S(2)}) collective-permute-start(bf16[1536,256]{1,0:T(8,128)(2,1)S(1)} %bitcast.306), channel_id=1, source_target_pairs={{0,4},{4,0},{1,5},{5,1},{2,6},{6,2},{3,7},{7,3},{8,12},{12,8},{9,1... | collective-permute-start | bytes 2359304 | tf_op jit(solution)/shard_map/ppermute | solution.py:135
  122.7 8.7 %collective-permute-start.8 = (bf16[16,32,256]{2,1,0:T(8,128)(2,1)S(1)}, bf16[16,32,256]{2,1,0:T(8,128)(2,1)S(1)}, u32[]{:S(2)}, u32[]{:S(2)}) collective-permute-start(bf16[16,32,256]{2,1,0:T(8,128)(2,1)S(1)} %bitcast.344), channel_id=1, source_target_pairs={{0,16},{16,0},{1,17},{17,1},{2,18},{18,2},{3,19},{19,3},{4,20},{20... | collective-permute-start | bytes 786440 | tf_op jit(solution)/shard_map/ppermute | solution.py:30
  (6 other events, 5.4 us)

commit v2 on v1

v2 whole, which is shorter than its diff:
```python
import jax
import jax.numpy as jnp
from jax import lax
from jax.sharding import PartitionSpec as P


GY = ("gy_hi", "core")


def silu_slope(values):
    sigma = jax.nn.sigmoid(values)
    return sigma * (1.0 + values * (1.0 - sigma))


DIMS = ("NHWC", "HWIO", "NHWC")


def conv(padded, kernel):
    return lax.conv_general_dilated(
        padded[None], kernel, (1, 1), "VALID", dimension_numbers=DIMS,
        preferred_element_type=jnp.float32,
    )[0]


def conv_back(padded, kernel):
    return conv(padded, jnp.swapaxes(kernel[::-1, ::-1], 2, 3))


def conv_slopes(padded, slope):
    return lax.conv_general_dilated(
        padded[None], slope[None], (1, 1), "VALID",
        dimension_numbers=("CHWN", "IHWO", "HWNC"), preferred_element_type=jnp.float32,
    )


def shifted(last, initial, axis):
    size = lax.axis_size(axis)
    up = [(i, i + 1) for i in range(size - 1)]
    down = [(j, i) for i, j in up]
    return lax.ppermute(last, axis, up), lax.ppermute(initial, axis, down)


def halo(tile, other, reach):
    rows, cols, channels = tile.shape

    def pack(a, b):
        return jnp.concatenate([a.reshape(-1, channels), b.reshape(-1, channels)], axis=0)

    before, after = shifted(
        pack(tile[rows - reach :], other[-1:]), pack(tile[:reach], other[:1]), GY
    )

    def opened(flat, shape, other_shape):
        size = shape[0] * shape[1]
        return flat[:size].reshape(shape), flat[size:].reshape(other_shape)

    shape, other_shape = (reach, cols, channels), (1,) + other.shape[1:]
    t_before, o_before = opened(before, shape, other_shape)
    t_after, o_after = opened(after, shape, other_shape)
    tile = jnp.concatenate([t_before, tile, t_after], axis=0)
    other = jnp.concatenate([o_before, other, o_after], axis=0)
    before, after = shifted(
        pack(tile[:, cols - reach :], other[:, -1:]), pack(tile[:, :reach], other[:, :1]), "gx"
    )
    shape, other_shape = (tile.shape[0], reach, channels), (other.shape[0], 1, other.shape[2])
    t_before, o_before = opened(before, shape, other_shape)
    t_after, o_after = opened(after, shape, other_shape)
    tile = jnp.concatenate([t_before, tile, t_after], axis=1)
    ring = [o_before, o_after, other[:1], other[-1:]]
    return tile, ring


def inside(count, margin, axis):
    where = lax.axis_index(axis) * count + lax.iota(jnp.int32, count + 2 * margin) - margin
    return (where >= 0) & (where < count * lax.axis_size(axis))


def swap_pairs(block, axis):
    return lax.ppermute(block, axis, [(0, 1), (1, 0)])


def reduce_all(first, proj, second):
    plane, line = ("section", "gy_hi"), "gx"
    planes = lax.axis_size("section") * lax.axis_size("gy_hi")
    lines = lax.axis_size(line)
    wide = proj.shape[1]
    flat_first = first.reshape(-1, first.shape[3])
    fold = wide // first.shape[3]
    seg = flat_first.shape[0] // fold
    folded = jnp.concatenate([flat_first[i * seg : (i + 1) * seg] for i in range(fold)], axis=1)
    flat_second = second.reshape(-1, wide)
    rows = [folded.shape[0], proj.shape[0], flat_second.shape[0]]
    total = sum(rows)
    unit = 2 * planes * lines * 16
    padded = -(-total // unit) * unit
    flat = jnp.concatenate(
        [flat_second, proj, folded, jnp.zeros((padded - total, wide), jnp.float32)], axis=0
    )
    half = padded // 2
    core = lax.axis_index("core")
    low, high = flat[:half], flat[half:]
    mine = jnp.where(core == 0, low, high)
    other = jnp.where(core == 0, high, low).astype(jnp.bfloat16)
    summed = mine + swap_pairs(other, "core").astype(jnp.float32)
    for axes, count in ((plane, planes), (line, lines)):
        parts = summed.astype(jnp.bfloat16).reshape(count, summed.shape[0] // count, wide)
        parts = lax.all_to_all(parts, axes, 0, 0, tiled=True)
        summed = parts.astype(jnp.float32).sum(axis=0)
    whole = summed.astype(jnp.bfloat16)
    for axes, count in ((line, lines), (plane, planes)):
        parts = jnp.broadcast_to(whole[None], (count,) + whole.shape)
        whole = lax.all_to_all(parts, axes, 0, 0, tiled=True).reshape(-1, wide)
    theirs = swap_pairs(whole, "core")
    low = jnp.where(core == 0, whole, theirs)
    high = jnp.where(core == 0, theirs, whole)
    flat = jnp.concatenate([low, high], axis=0).astype(jnp.float32)
    second = flat[: rows[2]].reshape(second.shape)
    proj = flat[rows[2] : rows[2] + rows[1]]
    folded = flat[rows[2] + rows[1] : total]
    width = first.shape[3]
    first = jnp.concatenate(
        [folded[:, i * width : (i + 1) * width] for i in range(fold)], axis=0
    ).reshape(first.shape)
    return first, proj, second


def per_device(images, first_kernel, projection, second_kernel, cotangent):
    image, upstream = images[0], cotangent[0]
    rows, cols, channels = image.shape
    half_rows, half_cols, wide = upstream.shape
    theirs = swap_pairs(upstream, "section")
    padded, ring = halo(image, upstream, 5)
    flat = jnp.concatenate([piece.reshape(-1, wide) for piece in ring], axis=0)
    flat = swap_pairs(flat, "section")
    pieces, at = [], 0
    for piece in ring:
        count = piece.shape[0] * piece.shape[1]
        pieces.append(flat[at : at + count].reshape(piece.shape))
        at += count
    left, right, top, bottom = pieces
    theirs = jnp.concatenate([top, theirs, bottom], axis=0)
    theirs = jnp.concatenate([left, theirs, right], axis=1)

    before = conv(padded, first_kernel)
    hidden = jax.nn.silu(before).astype(jnp.bfloat16)
    pooled = (
        hidden.astype(jnp.float32)
        .reshape(half_rows + 4, 2, half_cols + 4, 2, channels)
        .sum(axis=(1, 3))
        * 0.25
    ).astype(jnp.bfloat16)
    middle = jnp.einsum("ijc,cd->ijd", pooled, projection, preferred_element_type=jnp.float32)
    mask = inside(half_rows, 2, GY)[:, None] & inside(half_cols, 2, "gx")[None, :]
    middle = jnp.where(mask[:, :, None], middle, 0.0).astype(jnp.bfloat16)
    before_two = conv(middle, second_kernel)
    output = jax.nn.silu(before_two[1:-1, 1:-1]).astype(jnp.bfloat16)
    output = swap_pairs(output, "section")
    slope_two = (theirs.astype(jnp.float32) * silu_slope(before_two)).astype(jnp.bfloat16)
    own_slope = slope_two[1:-1, 1:-1]
    grad_second = conv_slopes(middle[1:-1, 1:-1], own_slope)
    back = conv_back(slope_two, second_kernel).astype(jnp.bfloat16)
    grad_projection = jnp.einsum(
        "ijc,ijd->cd", pooled[2:-2, 2:-2], back, preferred_element_type=jnp.float32
    )
    pooled_slope = jnp.einsum(
        "ijd,cd->ijc", back, projection, preferred_element_type=jnp.float32
    ).astype(jnp.bfloat16)
    spread = jnp.broadcast_to(
        (pooled_slope.astype(jnp.float32) * 0.25)[:, None, :, None, :],
        (half_rows, 2, half_cols, 2, channels),
    ).reshape(rows, cols, channels)
    slope = (spread * silu_slope(before[4:-4, 4:-4])).astype(jnp.bfloat16)
    grad_first = conv_slopes(padded[4:-4, 4:-4], slope)
    output, grad_first, grad_projection, grad_second = lax.optimization_barrier(
        (output, grad_first, grad_projection, grad_second)
    )
    grad_first, grad_projection, grad_second = reduce_all(
        grad_first, grad_projection, grad_second
    )
    return (output[None], grad_first, grad_projection, grad_second)


def solution(mesh):
    shape = dict(mesh.shape)
    grid = mesh.devices.reshape(shape["section"], shape["gy"] // 2, 2, shape["gx"])
    split = jax.sharding.Mesh(grid, ("section", "gy_hi", "core", "gx"))
    tiles = P("section", ("gy_hi", "core"), "gx", None)
    return jax.shard_map(
        per_device,
        mesh=split,
        in_specs=(tiles, P(), P(), P(), tiles),
        out_specs=(tiles, P(), P(), P()),
        check_vma=False,
    )
```

time: 136 us -> 123 us (0.904)
  starting transfers between devices: 33 us -> 14.2 us
  waiting for transfers between devices: 20.9 us -> 5.85 us
  local copies, waits for them, and re-layouts: 6.63 us -> 21 us
  other arithmetic: 8.58 us -> 14.2 us
    ppermute x14 -> x4, starting transfers between devices: 31.6 us -> 10.2 us  [shifted(): return (lax.ppermute(last, axis, up), lax.ppermute(initial, axis, down))]
    ppermute x14 -> x4, waiting for transfers between devices: 19 us -> 0.66 us  [shifted(): return (lax.ppermute(last, axis, up), lax.ppermute(initial, axis, down))]
    dot_general x48 -> x3, matrix products: 16.9 us -> 0.75 us  [the longest x1 0.27 us: per_device(): jnp.einsum('ijc,cd->ijd', pooled, projection, preferred_element_type=jnp....]
    conv_general_dilated x0 -> x5, matrix products: none -> 15.9 us  [the longest x2 10.8 us: conv_slopes(): lax.conv_general_dilated(padded[None], slope[None], (1, 1), 'VALID', dime...]
    unnamed x29 -> x50, local copies, waits for them, and re-layouts: 4.27 us -> 7.79 us
    ppermute x2 -> x5, waiting for transfers between devices: 1.91 us -> 5.18 us  [swap_pairs(): return lax.ppermute(block, axis, [(0, 1), (1, 0)])]
    broadcast_in_dim x0 -> x3, other arithmetic: none -> 2.85 us  [the longest x2 2.5 us: conv_slopes(): slope[None]]
    slice x8 -> x10, local copies, waits for them, and re-layouts: 1.71 us -> 4.44 us  [the longest x8 2.63 us: opened(): return (flat[:size].reshape(shape), flat[size:].reshape(other_shape))]
  transfers between devices with their start and end apart: 16 -> 9, of which waited for: 8 -> 5; matrix products, arithmetic and copies ran while one was open for 10% -> 30% of each run, Pallas kernels for 0% -> 0%
where the time goes in v2:
time: 123 us; the launch traced here: 122 us
  blocking collectives  48.5 us (39%)
  local copies, waits for them, and re-layouts  21 us (17%)
  matrix products  16.7 us (14%)
  other arithmetic  14.2 us (12%)
  starting transfers between devices  14.2 us (12%)
  waiting for transfers between devices  5.85 us (5%)
  between operations  1.36 us (1%)
    all_to_all x2, blocking collectives, reduce_all(): parts = lax.all_to_all(parts, axes, 0, 0, tiled=True)  27.4 us
    all_to_all x2, blocking collectives, reduce_all(): whole = lax.all_to_all(parts, axes, 0, 0, tiled=True).reshape(-1, wide)  21 us
    conv_general_dilated x2, matrix products, conv_slopes(): lax.conv_general_dilated(padded[None], slope[None], (1, 1), 'VALID', dime...  10.8 us
    ppermute x4, starting transfers between devices, shifted(): return (lax.ppermute(last, axis, up), lax.ppermute(initial, axis, down))  10.2 us
    unnamed x50, local copies, waits for them, and re-layouts  7.79 us
    ppermute x5, waiting for transfers between devices, swap_pairs(): return lax.ppermute(block, axis, [(0, 1), (1, 0)])  5.18 us
    conv_general_dilated x3, matrix products, conv(): lax.conv_general_dilated(padded[None], kernel, (1, 1), 'VALID', dimension...  5.09 us
    ppermute x5, starting transfers between devices, swap_pairs(): return lax.ppermute(block, axis, [(0, 1), (1, 0)])  4.01 us
  transfers between devices with their start and end apart: 9, of which 5 were waited for; matrix products, arithmetic and copies ran while one was open for 30% of the time, Pallas kernels for 0%

profile of v2, /device:TPU:0, one launch (start us, length us, event | category | flops | bytes accessed | tf_op | source)
XLA Modules:
  0.0 121.7 jit_solution(7290096276500250536)
XLA Ops:
  2.5 1.3 %collective-permute-start.1 = (bf16[384,128]{1,0:T(8,128)(2,1)S(1)}, bf16[384,128]{1,0:T(8,128)(2,1)S(1)}, u32[]{:S(2)}, u32[]{:S(2)}) collective-permute-start(bf16[384,128]{1,0:T(8,128)(2,1)S(1)} %pad_maximum_fusion.6), channel_id=1, source_target_pairs={{4,0},{8,4},{12,8},{5,1},{9,5},{13,9},{6,2},{10,6},{14,10},{7,3},{... | collective-permute-start | bytes 294920 | tf_op jit(solution)/shard_map/ppermute | solution.py:40
  3.8 3.0 %collective-permute-start = (bf16[384,128]{1,0:T(8,128)(2,1)S(1)}, bf16[384,128]{1,0:T(8,128)(2,1)S(1)}, u32[]{:S(2)}, u32[]{:S(2)}) collective-permute-start(bf16[384,128]{1,0:T(8,128)(2,1)S(1)} %pad_maximum_fusion.5), channel_id=1, source_target_pairs={{0,4},{4,8},{8,12},{1,5},{5,9},{9,13},{2,6},{6,10},{10,14},{3,7},{... | collective-permute-start | bytes 294920 | tf_op jit(solution)/shard_map/ppermute | solution.py:40
  6.9 1.8 %copy.141 = bf16[1,16,32,256]{3,1,2,0:T(8,128)(2,1)} copy(bf16[1,16,32,256]{3,2,1,0:T(8,128)(2,1)} %param.9) | data formatting | bytes 524288 | tf_op args[4]
  8.7 3.0 %collective-permute-start.6 = (bf16[16,32,256]{2,0,1:T(8,128)(2,1)}, bf16[16,32,256]{2,0,1:T(8,128)(2,1)}, u32[]{:S(2)}, u32[]{:S(2)}) collective-permute-start(bf16[16,32,256]{2,0,1:T(8,128)(2,1)} %bitcast.111), channel_id=1, source_target_pairs={{0,16},{16,0},{1,17},{17,1},{2,18},{18,2},{3,19},{19,3},{4,20},{20... | collective-permute-start | bytes 786440 | tf_op jit(solution)/shard_map/ppermute | solution.py:79
  12.8 1.3 %collective-permute-start.3 = (bf16[246,128]{1,0:T(8,128)(2,1)S(1)}, bf16[246,128]{1,0:T(8,128)(2,1)S(1)}, u32[]{:S(2)}, u32[]{:S(2)}) collective-permute-start(bf16[246,128]{1,0:T(8,128)(2,1)S(1)} %pad_maximum_fusion.11), channel_id=1, source_target_pairs={{1,0},{2,1},{3,2},{5,4},{6,5},{7,6},{9,8},{10,9},{11,10},{13,12},{... | collective-permute-start | bytes 188936 | tf_op jit(solution)/shard_map/ppermute | solution.py:40
  14.1 4.5 %collective-permute-start.2 = (bf16[246,128]{1,0:T(8,128)(2,1)S(1)}, bf16[246,128]{1,0:T(8,128)(2,1)S(1)}, u32[]{:S(2)}, u32[]{:S(2)}) collective-permute-start(bf16[246,128]{1,0:T(8,128)(2,1)S(1)} %pad_maximum_fusion.10), channel_id=1, source_target_pairs={{0,1},{1,2},{2,3},{4,5},{5,6},{6,7},{8,9},{9,10},{10,11},{12,13},{... | collective-permute-start | bytes 188936 | tf_op jit(solution)/shard_map/ppermute | solution.py:40
  22.6 2.1 %convolution_select_fusion = f32[40,8,10,128]{3,1,2,0:T(8,128)S(1)} fusion(bf16[3,3,128,128]{3,2,1,0:T(8,128)(2,1)S(1)} %copy-done.19, bf16[42,1,7,2,128]{4,2,3,0,1:T(8,128)(2,1)S(1)} %slice.160, bf16[42,1,8,10,128]{4,2,3,0,1:T(8,128)(2,1)S(1)} %copy.97, pred[8,10]{0,1:T(8,128)(4,1)S(1)} %copy-done.20), kind=kOutput, calls=%fused_computation.14 | convolution fusion | flops 947224576 | bytes 2944080 | tf_op jit(solution)/shard_map/conv_general_dilated | solution.py:19
  25.6 2.6 %convert_reduce_fusion = f32[20,36,128]{2,0,1:T(8,128)S(1)} fusion(f32[20,2,36,2,128]{4,1,0,3,2:T(2,128)S(1)} %bitcast.117), kind=kLoop, calls=%fused_computation.12 | loop fusion | flops 2488320 | bytes 1843200 | tf_op jit(solution)/shard_map/reduce_sum | solution.py:149
  30.0 2.0 %add_multiply_fusion = (f32[18,8,5,256]{3,1,2,0:T(8,128)}, f32[18,8,5,256]{3,1,2,0:T(8,128)S(1)}) fusion(bf16[3,3,256,256]{3,2,1,0:T(8,128)(2,1)S(1)} %copy-done, bf16[20,1,7,2,256]{4,2,3,0,1:T(8,128)(2,1)S(1)} %slice.162, bf16[20,1,8,5,256]{4,2,3,0,1:T(8,128)(2,1)S(1)} %copy.102, pred[8,5]{0,1:T(8,128)(4,1)S(1)} %copy-done.22), kind=kOutput, calls=%fused_computation.47 | convolution fusion | flops 852541440 | bytes 3207208 | tf_op jit(solution)/shard_map/conv_general_dilated | solution.py:19
  34.3 1.3 %slice.167 = bf16[36,128]{1,0:T(8,128)(2,1)} slice(bf16[246,128]{1,0:T(8,128)(2,1)} %copy-done.15), slice={[210:246], [0:128]} | slice | bytes 18432 | tf_op jit(solution)/shard_map/slice | solution.py:55
  35.6 1.3 %reshape_reshape.13 = bf16[18,256]{1,0:T(8,128)(2,1)} reshape(bf16[36,128]{1,0:T(8,128)(2,1)} %slice.167) | data formatting | bytes 18432 | tf_op jit(solution)/shard_map/reshape;reshape | solution.py:133
  36.9 1.3 %slice.166 = bf16[36,128]{1,0:T(8,128)(2,1)} slice(bf16[246,128]{1,0:T(8,128)(2,1)} %copy-done.16), slice={[210:246], [0:128]} | slice | bytes 18432 | tf_op jit(solution)/shard_map/slice | solution.py:55
  38.2 1.3 %reshape_reshape.12 = bf16[18,256]{1,0:T(8,128)(2,1)} reshape(bf16[36,128]{1,0:T(8,128)(2,1)} %slice.166) | data formatting | bytes 18432 | tf_op jit(solution)/shard_map/reshape;reshape | solution.py:133
  42.2 2.4 %collective-permute-done.5 = bf16[100,256]{1,0:T(8,128)(2,1)S(1)} collective-permute-done((bf16[100,256]{1,0:T(8,128)(2,1)S(1)}, bf16[100,256]{1,0:T(8,128)(2,1)S(1)}, u32[]{:S(2)}, u32[]{:S(2)}) %collective-permute-start.5) | collective-permute-done | bytes 51232 | tf_op jit(solution)/shard_map/ppermute | solution.py:79
  49.0 2.1 %fusion.49 = (bf16[1,16,32,256]{3,1,2,0:T(8,128)(2,1)}, bf16[16,32,256]{2,0,1:T(8,128)(2,1)}) fusion(f32[18,34,256]{2,0,1:T(8,128)S(1)} %copy-done.3, f32[18,34,256]{2,0,1:T(8,128)S(1)} %copy-done.2, bf16[18,1,256]{2,0,1:T(8,128)(2,1)S(1)} %get-tuple-element.47, bf16[1,32,256]{2,0,1:T(2,128)(2,1)S(1)} %copy.105, ...), kind=kLoop, calls=%fused_computation.81 | loop fusion | flops 2752512 | bytes 1886208 | tf_op jit(solution)/shard_map/broadcast_in_dim | solution.py:31
  52.5 7.4 %fusion.12 = f32[3,3,128,128]{3,2,1,0:T(8,128)} fusion(bf16[1,34,66,128]{3,2,1,0:T(8,128)(2,1)S(1)} %slice_bitcast_fusion.2, bf16[1,32,64,128]{3,1,2,0:T(8,128)(2,1)S(1)} %fusion.34), kind=kOutput, calls=%fused_computation.25 | convolution fusion | flops 603979776 | bytes 1688576 | tf_op jit(solution)/shard_map/conv_general_dilated | solution.py:30
  60.0 3.4 %fusion.25 = f32[3,3,256,256]{3,2,1,0:T(8,128)S(1)} fusion(bf16[1,18,34,256]{3,2,1,0:T(8,128)(2,1)S(1)} %copy-done.10, bf16[1,16,32,256]{3,1,2,0:T(8,128)(2,1)S(1)} %copy-done.11), kind=kOutput, calls=%fused_computation.49 | convolution fusion | flops 603979776 | bytes 2934784 | tf_op jit(solution)/shard_map/conv_general_dilated | solution.py:30
  64.7 2.3 %collective-permute-done.7 = bf16[1536,256]{1,0:T(8,128)(2,1)S(1)} collective-permute-done((bf16[1536,256]{1,0:T(8,128)(2,1)S(1)}, bf16[1536,256]{1,0:T(8,128)(2,1)S(1)}, u32[]{:S(2)}, u32[]{:S(2)}) %collective-permute-start.7) | collective-permute-done | bytes 786464 | tf_op jit(solution)/shard_map/ppermute | solution.py:79
  67.4 15.2 %all_to_all.20 = bf16[4,384,256]{2,1,0:T(8,128)(2,1)S(1)} all-to-all(bf16[4,384,256]{2,1,0:T(8,128)(2,1)S(1)} %bitcast.124), channel_id=1, replica_groups=mesh['section'=2,'gy_hi'=2,'core'=2,'gx'=4] {'section','gy_hi'}, dimensions={0} | all-to-all | bytes 1572864 | tf_op jit(solution)/shard_map/all_to_all | solution.py:107
  82.7 12.2 %all_to_all.21 = bf16[4,96,256]{2,1,0:T(8,128)(2,1)S(1)} all-to-all(bf16[4,96,256]{2,1,0:T(8,128)(2,1)S(1)} %bitcast.137), channel_id=1, replica_groups=mesh['section'=2,'gy_hi'=2,'core'=2,'gx'=4] {'gx'}, dimensions={0} | all-to-all | bytes 393216 | tf_op jit(solution)/shard_map/all_to_all | solution.py:107
  95.0 9.2 %all_to_all.22 = bf16[4,96,256]{2,1,0:T(8,128)(2,1)S(1)} all-to-all(bf16[4,96,256]{2,1,0:T(8,128)(2,1)S(1)} %broadcast_in_dim.70), channel_id=1, replica_groups=mesh['section'=2,'gy_hi'=2,'core'=2,'gx'=4] {'gx'}, dimensions={0} | all-to-all | bytes 393216 | tf_op jit(solution)/shard_map/all_to_all | solution.py:112
  104.3 11.9 %all_to_all.23 = bf16[4,384,256]{2,1,0:T(8,128)(2,1)S(1)} all-to-all(bf16[4,384,256]{2,1,0:T(8,128)(2,1)S(1)} %broadcast_in_dim.72), channel_id=1, replica_groups=mesh['section'=2,'gy_hi'=2,'core'=2,'gx'=4] {'section','gy_hi'}, dimensions={0} | all-to-all | bytes 1572864 | tf_op jit(solution)/shard_map/all_to_all | solution.py:112
  116.1 1.7 %copy.118 = bf16[1,16,32,256]{3,2,1,0:T(8,128)(2,1)} copy(bf16[1,16,32,256]{3,1,2,0:T(8,128)(2,1)} %bitcast.38) | data formatting | bytes 524288
  119.3 1.6 %fusion.9 = f32[2304,256]{1,0:T(8,128)} fusion(bf16[1536,256]{1,0:T(8,128)(2,1)S(1)} %get-tuple-element.33, bf16[1536,256]{1,0:T(8,128)(2,1)S(1)} %get-tuple-element.32), kind=kLoop, calls=%fused_computation.21 | loop fusion | flops 2359296 | bytes 3932160 | tf_op jit(solution)/shard_map/convert_element_type | solution.py:116
  (138 shorter events, 24.2 us)
Async XLA Ops:
  0.6 29.3 %copy-start = (bf16[3,3,256,256]{3,2,1,0:T(8,128)(2,1)S(1)}, bf16[3,3,256,256]{3,2,1,0:T(8,128)(2,1)}, u32[]{:S(2)}) copy-start(bf16[3,3,256,256]{3,2,1,0:T(8,128)(2,1)} %param.8) | copy-start | bytes 3538948
  0.6 11.2 %copy-start.1 = (bf16[1,32,64,128]{3,2,1,0:T(8,128)(2,1)S(1)}, bf16[1,32,64,128]{3,2,1,0:T(8,128)(2,1)}, u32[]{:S(2)}) copy-start(bf16[1,32,64,128]{3,2,1,0:T(8,128)(2,1)} %param.5) | copy-start | bytes 1572868
  2.5 9.2 %collective-permute-start.1 = (bf16[384,128]{1,0:T(8,128)(2,1)S(1)}, bf16[384,128]{1,0:T(8,128)(2,1)S(1)}, u32[]{:S(2)}, u32[]{:S(2)}) collective-permute-start(bf16[384,128]{1,0:T(8,128)(2,1)S(1)} %pad_maximum_fusion.6), channel_id=1, source_target_pairs={{4,0},{8,4},{12,8},{5,1},{9,5},{13,9},{6,2},{10,6},{14,10},{7,3},{... | collective-permute-start | bytes 294920 | tf_op jit(solution)/shard_map/ppermute | solution.py:40
  3.8 7.9 %collective-permute-start = (bf16[384,128]{1,0:T(8,128)(2,1)S(1)}, bf16[384,128]{1,0:T(8,128)(2,1)S(1)}, u32[]{:S(2)}, u32[]{:S(2)}) collective-permute-start(bf16[384,128]{1,0:T(8,128)(2,1)S(1)} %pad_maximum_fusion.5), channel_id=1, source_target_pairs={{0,4},{4,8},{8,12},{1,5},{5,9},{9,13},{2,6},{6,10},{10,14},{3,7},{... | collective-permute-start | bytes 294920 | tf_op jit(solution)/shard_map/ppermute | solution.py:40
  8.7 36.0 %collective-permute-start.6 = (bf16[16,32,256]{2,0,1:T(8,128)(2,1)}, bf16[16,32,256]{2,0,1:T(8,128)(2,1)}, u32[]{:S(2)}, u32[]{:S(2)}) collective-permute-start(bf16[16,32,256]{2,0,1:T(8,128)(2,1)} %bitcast.111), channel_id=1, source_target_pairs={{0,16},{16,0},{1,17},{17,1},{2,18},{18,2},{3,19},{19,3},{4,20},{20... | collective-permute-start | bytes 786440 | tf_op jit(solution)/shard_map/ppermute | solution.py:79
  12.8 6.7 %collective-permute-start.3 = (bf16[246,128]{1,0:T(8,128)(2,1)S(1)}, bf16[246,128]{1,0:T(8,128)(2,1)S(1)}, u32[]{:S(2)}, u32[]{:S(2)}) collective-permute-start(bf16[246,128]{1,0:T(8,128)(2,1)S(1)} %pad_maximum_fusion.11), channel_id=1, source_target_pairs={{1,0},{2,1},{3,2},{5,4},{6,5},{7,6},{9,8},{10,9},{11,10},{13,12},{... | collective-permute-start | bytes 188936 | tf_op jit(solution)/shard_map/ppermute | solution.py:40
  14.1 6.6 %collective-permute-start.2 = (bf16[246,128]{1,0:T(8,128)(2,1)S(1)}, bf16[246,128]{1,0:T(8,128)(2,1)S(1)}, u32[]{:S(2)}, u32[]{:S(2)}) collective-permute-start(bf16[246,128]{1,0:T(8,128)(2,1)S(1)} %pad_maximum_fusion.10), channel_id=1, source_target_pairs={{0,1},{1,2},{2,3},{4,5},{5,6},{6,7},{8,9},{9,10},{10,11},{12,13},{... | collective-permute-start | bytes 188936 | tf_op jit(solution)/shard_map/ppermute | solution.py:40
  21.7 1.0 copy-start.19
  25.5 2.7 %copy-start.17 = (bf16[128,256]{1,0:T(8,128)(2,1)S(1)}, bf16[128,256]{1,0:T(8,128)(2,1)}, u32[]{:S(2)}) copy-start(bf16[128,256]{1,0:T(8,128)(2,1)} %param.7) | copy-start | bytes 196612
  29.0 1.0 copy-start.22
  39.5 1.6 %copy-start.5 = (bf16[20,36,256]{2,1,0:T(8,128)(2,1)S(1)}, bf16[20,36,256]{2,1,0:T(8,128)(2,1)}, u32[]{:S(2)}) copy-start(bf16[20,36,256]{2,1,0:T(8,128)(2,1)} %copy-done.4) | copy-start | bytes 1105924
  39.5 2.4 %copy-start.8 = (f32[18,8,5,256]{3,1,2,0:T(8,128)S(1)}, f32[18,8,5,256]{3,1,2,0:T(8,128)}, u32[]{:S(2)}) copy-start(f32[18,8,5,256]{3,1,2,0:T(8,128)} %get-tuple-element.52) | copy-start | bytes 2211844
  40.4 4.2 %collective-permute-start.5 = (bf16[100,256]{1,0:T(8,128)(2,1)S(1)}, bf16[100,256]{1,0:T(8,128)(2,1)S(1)}, u32[]{:S(2)}, u32[]{:S(2)}) collective-permute-start(bf16[100,256]{1,0:T(8,128)(2,1)S(1)} %pad_maximum_fusion.12), channel_id=1, source_target_pairs={{0,16},{16,0},{1,17},{17,1},{2,18},{18,2},{3,19},{19,3},{4,20},{20... | collective-permute-start | bytes 153608 | tf_op jit(solution)/shard_map/ppermute | solution.py:79
  46.5 1.8 %copy-start.18 = (bf16[128,256]{1,0:T(8,128)(2,1)S(1)}, bf16[128,256]{1,0:T(8,128)(2,1)}, u32[]{:S(2)}) copy-start(bf16[128,256]{1,0:T(8,128)(2,1)} %param.7) | copy-start | bytes 196612
  47.5 1.4 %copy-start.2 = (f32[18,34,256]{2,0,1:T(8,128)S(1)}, f32[18,34,256]{2,0,1:T(8,128)}, u32[]{:S(2)}) copy-start(f32[18,34,256]{2,0,1:T(8,128)} %add_divide_fusion) | copy-start | bytes 1880068
  47.5 1.5 %copy-start.3 = (f32[18,34,256]{2,0,1:T(8,128)S(1)}, f32[18,34,256]{2,0,1:T(8,128)}, u32[]{:S(2)}) copy-start(f32[18,34,256]{2,0,1:T(8,128)} %slice_bitcast_fusion.1) | copy-start | bytes 1880068
  51.1 12.6 %collective-permute-start.4 = (bf16[16,32,256]{2,0,1:T(8,128)(2,1)}, bf16[16,32,256]{2,0,1:T(8,128)(2,1)}, u32[]{:S(2)}, u32[]{:S(2)}) collective-permute-start(bf16[16,32,256]{2,0,1:T(8,128)(2,1)} %get-tuple-element.35), channel_id=1, source_target_pairs={{0,16},{16,0},{1,17},{17,1},{2,18},{18,2},{3,19},{19,3},{4,20},{20... | collective-permute-start | bytes 786440 | tf_op jit(solution)/shard_map/ppermute | solution.py:79
  52.5 7.5 %copy-start.10 = (bf16[1,18,34,256]{3,2,1,0:T(8,128)(2,1)S(1)}, bf16[1,18,34,256]{3,2,1,0:T(8,128)(2,1)}, u32[]{:S(2)}) copy-start(bf16[1,18,34,256]{3,2,1,0:T(8,128)(2,1)} %slice_bitcast_fusion.3) | copy-start | bytes 940036
  52.5 7.5 %copy-start.11 = (bf16[1,16,32,256]{3,1,2,0:T(8,128)(2,1)S(1)}, bf16[1,16,32,256]{3,1,2,0:T(8,128)(2,1)}, u32[]{:S(2)}) copy-start(bf16[1,16,32,256]{3,1,2,0:T(8,128)(2,1)} %get-tuple-element.34) | copy-start | bytes 786436
  59.9 3.4 %copy-start.7 = (bf16[16,1,32,256]{3,0,2,1:T(8,128)(2,1)S(1)}, bf16[16,1,32,256]{3,0,2,1:T(8,128)(2,1)}, u32[]{:S(2)}) copy-start(bf16[16,1,32,256]{3,0,2,1:T(8,128)(2,1)} %copy-done.6) | copy-start | bytes 786436
  59.9 3.4 %copy-start.13 = (bf16[20,36,128]{2,1,0:T(8,128)(2,1)S(1)}, bf16[20,36,128]{2,1,0:T(8,128)(2,1)}, u32[]{:S(2)}) copy-start(bf16[20,36,128]{2,1,0:T(8,128)(2,1)} %copy-done.12) | copy-start | bytes 552964
  60.0 3.7 %copy-start.9 = (f32[3,3,128,128]{3,2,1,0:T(8,128)S(1)}, f32[3,3,128,128]{3,2,1,0:T(8,128)}, u32[]{:S(2)}) copy-start(f32[3,3,128,128]{3,2,1,0:T(8,128)} %fusion.12) | copy-start | bytes 1769476
  64.7 2.4 %collective-permute-start.7 = (bf16[1536,256]{1,0:T(8,128)(2,1)S(1)}, bf16[1536,256]{1,0:T(8,128)(2,1)S(1)}, u32[]{:S(2)}, u32[]{:S(2)}) collective-permute-start(bf16[1536,256]{1,0:T(8,128)(2,1)S(1)} %fusion.5), channel_id=1, source_target_pairs={{0,4},{4,0},{1,5},{5,1},{2,6},{6,2},{3,7},{7,3},{8,12},{12,8},{9,1... | collective-permute-start | bytes 2359304 | tf_op jit(solution)/shard_map/ppermute | solution.py:79
  116.1 2.3 %collective-permute-start.8 = (bf16[1536,256]{1,0:T(8,128)(2,1)S(1)}, bf16[1536,256]{1,0:T(8,128)(2,1)S(1)}, u32[]{:S(2)}, u32[]{:S(2)}) collective-permute-start(bf16[1536,256]{1,0:T(8,128)(2,1)S(1)} %bitcast.125), channel_id=1, source_target_pairs={{0,4},{4,0},{1,5},{5,1},{2,6},{6,2},{3,7},{7,3},{8,12},{12,8},{9,1... | collective-permute-start | bytes 2359304 | tf_op jit(solution)/shard_map/ppermute | solution.py:79
  (8 other events, 5.8 us)

commit v3 on v0

v3 whole, which is shorter than its diff:
```python
import functools
import math

import jax
import jax.numpy as jnp
from jax import lax
from jax.experimental import pallas as pl
from jax.experimental.pallas import tpu as pltpu
from jax.sharding import PartitionSpec as P

F32, BF16 = jnp.float32, jnp.bfloat16
NT, TN = (((1,), (1,)), ((), ())), (((0,), (0,)), ((), ()))
SIDE, EDGE, REACH = 8, 48, 5
GY, GX = ("gy_hi", "core"), ("gx_hi", "gx_lo")
PLANE = ("section", "gy_hi", "gx_lo")


def dot(left, right):
    return jnp.dot(left, right, preferred_element_type=F32)


def sloped(values):
    sigma = 1.0 / (1.0 + jnp.exp(-values))
    return sigma * (1.0 + values * (1.0 - sigma))


def silu(values):
    return values / (1.0 + jnp.exp(-values))


def spread_taps(value, out, lanes):
    cols = value.shape[1]
    out[..., 0:lanes] = pltpu.roll(value, 1, 1).astype(BF16)
    out[..., lanes : 2 * lanes] = value.astype(BF16)
    out[..., 2 * lanes : 3 * lanes] = pltpu.roll(value, cols - 1, 1).astype(BF16)


def sides(even, odd, axes):
    place, first = lax.axis_index(axes), lax.axis_index(axes[1]) == 0
    even, odd = even.astype(F32), odd.astype(F32)
    lower, upper = jnp.where(first, odd, even), jnp.where(first, even, odd)
    lower = jnp.where(place == 0, 0.0, lower)
    return lower, jnp.where(place == lax.axis_size(axes) - 1, 0.0, upper)


def forward_kernel(
    tile, rows_even, rows_odd, cols_even, cols_odd, first_kernel, projection, second_kernel,
    features, taps_one, field_one, taps_mid, field_two, pool, weights_one, sums,
):
    rows, cols, lanes = tile.shape
    half_rows, half_cols, wide = features.shape
    pitch = cols + 2 * SIDE
    reach = rows_even.shape[0] - 1
    tall = rows + 2 * reach
    above, below = sides(rows_even[0:reach], rows_odd[0:reach], GY)
    body = jnp.concatenate([above, tile[...].astype(F32), below], axis=0)
    before, after = sides(cols_even[0 : tall * SIDE], cols_odd[0 : tall * SIDE], GX)
    before, after = [side.reshape(tall, SIDE, lanes) for side in (before, after)]
    full = jnp.concatenate([body, after, before], axis=1)
    spread_taps(full, taps_one, lanes)
    for row in range(4):
        at = row * 3 * lanes
        zero = jnp.zeros((3 * lanes, lanes), BF16)
        left = first_kernel[row].reshape(3 * lanes, lanes) if row < 3 else zero
        right = first_kernel[row - 1].reshape(3 * lanes, lanes) if row else zero
        weights_one[at : at + 3 * lanes, 0:lanes] = left
        weights_one[at : at + 3 * lanes, lanes : 2 * lanes] = right
    pairs = half_rows + 4
    step = 10 if pairs % 10 == 0 else pairs

    def first(index, carry):
        pair = index * step
        picked = [
            taps_one[pl.ds(2 * pair + row // 2 * 2, 2 * step)]
            .reshape(step, 2, pitch, 3 * lanes)[:, row % 2]
            .reshape(step * pitch, 3 * lanes)
            for row in range(4)
        ]
        value = dot(jnp.concatenate(picked, axis=1), weights_one[...])
        field_one[pl.ds(pair, step)] = value.reshape(step, pitch, 2 * lanes)
        hidden = silu(value).astype(BF16).astype(F32)
        at = pl.multiple_of(pair * pitch, 8)
        sums[pl.ds(at, step * pitch), :] = hidden[:, :lanes] + hidden[:, lanes:]
        return carry

    lax.fori_loop(0, pairs // step, first, 0)
    half_pitch = pitch // 2
    cells = pairs * half_pitch
    pooled = (
        0.25 * (sums[pl.ds(0, cells, stride=2), :] + sums[pl.ds(1, cells, stride=2), :])
    ).astype(BF16)
    own_pool = pooled.astype(F32).reshape(pairs, half_pitch, lanes)
    pool[...] = own_pool[2 : half_rows + 2, 0:half_cols].astype(BF16)
    middle = dot(pooled, projection[...]).reshape(pairs, half_pitch, wide)
    row = lax.broadcasted_iota(jnp.int32, middle.shape, 0)
    col = lax.broadcasted_iota(jnp.int32, middle.shape, 1)
    gy, gx = lax.axis_index(GY), lax.axis_index(GX)
    low = jnp.where(gy == 0, 2, 0)
    high = jnp.where(gy == lax.axis_size(GY) - 1, pairs - 2, pairs)
    right = jnp.where(gx == lax.axis_size(GX) - 1, half_cols, half_cols + SIDE // 2)
    left = jnp.where(gx == 0, half_pitch, half_cols + SIDE // 2)
    keep = (row >= low) & (row < high) & ((col < right) | (col >= left))
    middle = jnp.where(keep, middle, 0.0)
    middle = jnp.concatenate([middle, middle[:, half_pitch - 8 :]], axis=1)
    spread_taps(middle, taps_mid, wide)
    pitch_two = half_pitch + 8
    outs = half_rows + 2
    part = outs

    def second(index, carry):
        at = index * part
        picked = [
            taps_mid[pl.ds(at + row, part)].reshape(part * pitch_two, 3 * wide) for row in range(3)
        ]
        value = dot(
            jnp.concatenate(picked, axis=1), second_kernel[...].reshape(9 * wide, wide)
        )
        field_two[pl.ds(at, part)] = value.reshape(part, pitch_two, wide)
        return carry

    lax.fori_loop(0, outs // part, second, 0)
    features[...] = silu(field_two[1 : half_rows + 1, 0:half_cols]).astype(BF16)


def split_halves(flat, mine, other, chunk):
    half, core, flip = mine.shape[0], lax.axis_index("core"), lax.axis_index(GX[0])
    count = half // chunk if chunk else 1
    size = half // count
    for block in range(count):
        place = flip * (1 - 2 * (block % 2)) + block if chunk else 0
        at = pl.ds(block * size, size)
        for target, owner in ((mine, core), (other, 1 - core)):
            start = pl.multiple_of(owner * half + place * size, 64)
            target[at, :] = flat[pl.ds(start, size), :]


def backward_kernel(
    chunk, theirs, ring, taps_one, field_one, taps_mid, field_two, pool, projection, second_kernel,
    mine, other, cot, taps_slope, up, flat,
):
    half_rows, half_cols, wide = theirs.shape
    lanes = projection.shape[0]
    rows, cols, pitch = 2 * half_rows, 2 * half_cols, taps_one.shape[1]
    outs, pitch_two = field_two.shape[:2]
    cot[...] = jnp.zeros(cot.shape, F32)
    cot[1 : half_rows + 1, 0:half_cols] = theirs[...].astype(F32)
    top, bottom = sides(ring[0:cols], ring[cols : 2 * cols], GY)
    at = 2 * cols
    left, right = sides(ring[at : at + EDGE], ring[at + EDGE : at + 2 * EDGE], GX)
    for part in range(2):
        lane = slice(part * lanes, (part + 1) * lanes)
        at = part * half_cols
        cot[0, 0:half_cols, lane] = top[at : at + half_cols]
        cot[half_rows + 1, 0:half_cols, lane] = bottom[at : at + half_cols]
        at = part * (EDGE // 2)
        cot[:, pitch_two - 1 : pitch_two, lane] = left[at : at + outs].reshape(outs, 1, lanes)
        cot[:, half_cols : half_cols + 1, lane] = right[at : at + outs].reshape(outs, 1, lanes)
    slope_two = cot[...] * sloped(field_two[...])
    spread_taps(slope_two, taps_slope, wide)
    own = half_rows * half_cols
    own_slope = slope_two[1 : half_rows + 1, 0:half_cols].reshape(own, wide).astype(BF16)
    for row in range(3):
        window = taps_mid[row + 1 : row + 1 + half_rows, 0:half_cols].reshape(own, 3 * wide)
        grad = lax.dot_general(window, own_slope, TN, preferred_element_type=F32)
        for col in range(3):
            at = (row * 3 + col) * wide
            flat[at : at + wide, :] = grad[col * wide : (col + 1) * wide].astype(BF16)
    windows = [
        taps_slope[row : row + half_rows, 0:half_cols].reshape(own, 3 * wide) for row in range(3)
    ]
    kernels = [second_kernel[2 - row, 2 - col] for row in range(3) for col in range(3)]
    kernels = jnp.concatenate(kernels, axis=1)
    windows = jnp.concatenate(windows, axis=1)
    cut = own // 2
    back = [
        lax.dot_general(windows[at : at + cut], kernels, NT, preferred_element_type=F32)
        for at in (0, cut)
    ]
    back = jnp.concatenate(back, axis=0).astype(BF16)
    at = 9 * wide
    flat[at : at + lanes, :] = dot(pool[...].astype(F32).reshape(own, lanes).T.astype(BF16), back).astype(BF16)
    at += lanes
    down = lax.dot_general(back, projection[...], NT, preferred_element_type=F32)
    down = down.astype(BF16).astype(F32) * 0.25
    up[pl.ds(0, own, stride=2), :] = down
    up[pl.ds(1, own, stride=2), :] = down
    cells = 2 * own
    field = field_one[2 : half_rows + 2, 0:cols].reshape(cells, 2 * lanes)
    slope_one = jnp.concatenate([up[...], up[...]], axis=1) * sloped(field)
    slope_one = slope_one.astype(BF16)
    grads = []
    for row in range(4):
        start = REACH - 1 + row
        window = taps_one[start : start + rows].reshape(half_rows, 2, pitch, 3 * lanes)[:, 0, 0:cols]
        window = window.reshape(cells, 3 * lanes)
        grads.append(lax.dot_general(window, slope_one, TN, preferred_element_type=F32))
    for tap in range(9):
        row, col = tap // 3, tap % 3
        span = slice(col * lanes, (col + 1) * lanes)
        grad = grads[row][span, :lanes] + grads[row + 1][span, lanes:]
        top = at + (tap % 4) * lanes + (4 * lanes if tap == 8 else 0)
        side = lanes if 4 <= tap < 8 else 0
        flat[top : top + lanes, side : side + lanes] = grad.astype(BF16)
    top = at + 4 * lanes
    flat[top : top + lanes, lanes : 2 * lanes] = jnp.zeros((lanes, lanes), BF16)
    used = at + 5 * lanes
    total = flat.shape[0]
    if used < total:
        flat[used:total, :] = jnp.zeros((total - used, wide), BF16)
    split_halves(flat, mine, other, chunk)


def resident(*arrays):
    return [pltpu.with_memory_space_constraint(array, pltpu.VMEM) for array in arrays]


def forward(tile, halo, first_kernel, projection, second_kernel):
    rows, cols, lanes = tile.shape
    half_rows, half_cols, wide = rows // 2, cols // 2, projection.shape[1]
    pitch = cols + 2 * SIDE
    pitch_two = pitch // 2 + 8
    vmem = pl.BlockSpec(memory_space=pltpu.VMEM)
    return pl.pallas_call(
        forward_kernel,
        out_shape=(
            pltpu.VMEM((half_rows, half_cols, wide), BF16),
            pltpu.VMEM((rows + 2 * REACH, pitch, 3 * lanes), BF16),
            pltpu.VMEM((half_rows + 4, pitch, 2 * lanes), F32),
            pltpu.VMEM((half_rows + 4, pitch_two, 3 * wide), BF16),
            pltpu.VMEM((half_rows + 2, pitch_two, wide), F32),
            pltpu.VMEM((half_rows, half_cols, lanes), BF16),
        ),
        in_specs=[vmem] * 8,
        out_specs=(vmem,) * 6,
        scratch_shapes=[
            pltpu.VMEM((12 * lanes, 2 * lanes), BF16),
            pltpu.VMEM(((half_rows + 4) * pitch, lanes), F32),
        ],
        compiler_params=pltpu.CompilerParams(vmem_limit_bytes=20 << 20),
    )(
        *resident(tile, *halo, first_kernel, projection, second_kernel),
    )


def backward(theirs, ring, kept, projection, second_kernel, total, chunk):
    half_rows, half_cols, wide = theirs.shape
    outs, pitch_two = kept[3].shape[:2]
    lanes = projection.shape[0]
    vmem = pl.BlockSpec(memory_space=pltpu.VMEM)
    return pl.pallas_call(
        functools.partial(backward_kernel, chunk),
        out_shape=(
            pltpu.VMEM((total // 2, wide), BF16),
            pltpu.VMEM((total // 2, wide), BF16),
        ),
        in_specs=[vmem] * 9,
        out_specs=(vmem,) * 2,
        scratch_shapes=[
            pltpu.VMEM((outs, pitch_two, wide), F32),
            pltpu.VMEM((outs, pitch_two, 3 * wide), BF16),
            pltpu.VMEM((4 * half_rows * half_cols // 2, lanes), F32),
            pltpu.VMEM((total, wide), BF16),
        ],
        compiler_params=pltpu.CompilerParams(vmem_limit_bytes=24 << 20),
    )(*resident(theirs, ring, *kept, projection, second_kernel))


def unpack_half(own, chunk, source, grads, held, sent):
    first, projection, second = grads
    lanes, wide = projection.shape
    half, flip = source.shape[0], lax.axis_index(GX[0])
    low = lax.axis_index("core") == (0 if own else 1)
    piece = math.gcd(64, chunk) if chunk else lanes
    jobs = []

    def send(rows, side, target):
        at, inside = rows[0] % half, rows[0] < half
        slot = sent.at[len(jobs)]
        span = slice(at, at + rows[1])
        here = low if inside else jnp.logical_not(low)

        @pl.when(here)
        def _():
            for step in range(at, at + rows[1], piece):
                start = step
                if chunk:
                    start = step + flip * (1 - 2 * (step // chunk % 2)) * chunk
                    start = pl.multiple_of(start, piece)
                held[step : step + piece, side] = source[pl.ds(start, piece), side].astype(F32)
            pltpu.make_async_copy(held.at[span, side], target, slot).start()

        jobs.append((here, held.at[span, side], target, slot))

    whole = slice(0, wide)
    for tap in range(9):
        send((tap * wide, wide), whole, second.at[tap // 3, tap % 3])
    at = 9 * wide
    send((at, lanes), whole, projection)
    at += lanes
    for tap in range(9):
        top = at + (tap % 4) * lanes + (4 * lanes if tap == 8 else 0)
        side = lanes if 4 <= tap < 8 else 0
        send((top, lanes), slice(side, side + lanes), first.at[tap // 3, tap % 3])
    for here, origin, target, slot in jobs:

        @pl.when(here)
        def _(origin=origin, target=target, slot=slot):
            pltpu.make_async_copy(origin, target, slot).wait()


def unpack_own(chunk, source, first, projection, second, held, sent):
    unpack_half(True, chunk, source, (first, projection, second), held, sent)


def unpack_other(
    chunk, source, features, first_in, projection_in, second_in, output, first, projection, second,
    held, sent,
):
    copy = pltpu.make_async_copy(features, output, sent.at[19])
    copy.start()
    unpack_half(False, chunk, source, (first, projection, second), held, sent)
    copy.wait()


def unpack_call(kernel, chunk, arrays, outs, aliases):
    vmem, hbm = pl.BlockSpec(memory_space=pltpu.VMEM), pl.BlockSpec(memory_space=pl.ANY)
    resting = len(aliases)
    moving = resident(*arrays[: len(arrays) - resting])
    return pl.pallas_call(
        functools.partial(kernel, chunk),
        out_shape=outs,
        in_specs=[vmem] * len(moving) + [hbm] * resting,
        out_specs=(hbm,) * len(outs),
        scratch_shapes=[
            pltpu.VMEM(arrays[0].shape, F32),
            pltpu.SemaphoreType.DMA((20,)),
        ],
        input_output_aliases=aliases,
        compiler_params=pltpu.CompilerParams(vmem_limit_bytes=12 << 20),
    )(*moving, *arrays[len(arrays) - resting :])


def swap_pairs(block, axis):
    return lax.ppermute(block, axis, [(0, 1), (1, 0)])


def swap_neighbours(even, odd, axes, spare):
    size, others = lax.axis_size(axes), lax.axis_size(spare)
    near = [(i, i + 1) for i in range(0, size, 2)]
    far = [(i, i + 1) for i in range(1, size - 1, 2)]
    leading = spare == "gy_hi"

    def place(i, at):
        return at * size + i if leading else i * others + at

    far = [(place(i, at), place(j, at)) for i, j in far for at in range(others)]
    ends = [(i, at) for i in (0, size - 1) for at in range(0, others, 2)]
    far += [(place(i, at), place(i, at + 1)) for i, at in ends]
    names = (spare,) + axes if leading else axes + (spare,)

    def both(pairs):
        return [pair for i, j in pairs for pair in ((i, j), (j, i))]

    odd = lax.ppermute(odd, names, both(far))
    even = lax.ppermute(even, axes, both(near))
    return even, odd


def edges_kernel(
    image, upstream, rows_even, rows_odd, tile_even, tile_odd, strip_even, strip_odd, sent,
):
    rows, cols, lanes = image.shape
    half_rows, half_cols, _ = upstream.shape
    lower, left = lax.axis_index("core") == 0, lax.axis_index("gx_lo") == 0
    copies = []

    def send(source, target):
        copy = pltpu.make_async_copy(source, target, sent.at[len(copies)])
        copy.start()
        copies.append(copy)

    for target, at_end in ((rows_odd, ~lower), (rows_even, lower)):
        start = jnp.where(at_end, rows - REACH, 0)
        row = jnp.where(at_end, half_rows - 1, 0)
        send(image.at[pl.ds(start, REACH)], target.at[0:REACH])
        for part in range(2):
            send(
                upstream.at[row, :, part * lanes : (part + 1) * lanes],
                target.at[REACH, part * half_cols : (part + 1) * half_cols],
            )
    for target, strip, at_end in ((tile_odd, strip_odd, ~left), (tile_even, strip_even, left)):
        start = pl.multiple_of(jnp.where(at_end, cols - SIDE, 0), SIDE)
        cell = pl.multiple_of(jnp.where(at_end, half_cols - SIDE, 0), SIDE)
        send(image.at[:, pl.ds(start, SIDE)], target)
        send(upstream.at[:, pl.ds(cell, SIDE)], strip)
    for copy in copies:
        copy.wait()


def edges(image, upstream):
    hbm, vmem = pl.BlockSpec(memory_space=pl.ANY), pl.BlockSpec(memory_space=pltpu.VMEM)
    rows, cols, lanes = image.shape
    half_rows, _, wide = upstream.shape
    shapes = [(REACH + 1, cols, lanes), (rows, SIDE, lanes), (half_rows, SIDE, wide)]
    return pl.pallas_call(
        edges_kernel,
        out_shape=[pltpu.VMEM(shape, BF16) for shape in shapes for _ in range(2)],
        in_specs=[hbm, hbm],
        out_specs=[vmem] * 6,
        scratch_shapes=[pltpu.SemaphoreType.DMA((10,))],
        compiler_params=pltpu.CompilerParams(vmem_limit_bytes=4 << 20),
    )(*[pltpu.with_memory_space_constraint(array, pltpu.HBM) for array in (image, upstream)])


def columns_kernel(
    rows_even, rows_odd, tile_even, tile_odd, strip_even, strip_odd, even, odd, edge
):
    rows, side, lanes = tile_even.shape
    half_rows = strip_even.shape[0]
    cols = rows_even.shape[1]
    half_cols = cols // 2
    tall = rows + 2 * REACH
    left = lax.axis_index("gx_lo") == 0
    above, below = sides(rows_even[...], rows_odd[...], GY)
    for target, tile, strip, at_end in (
        (odd, tile_odd, strip_odd, ~left), (even, tile_even, strip_even, left),
    ):

        def near(block):
            return jnp.where(at_end, block[0:REACH, cols - side :], block[0:REACH, 0:side])

        body = jnp.concatenate([near(above), tile[...].astype(F32), near(below)], axis=0)
        target[0 : tall * side] = body.reshape(tall * side, lanes).astype(BF16)
        edge[...] = jnp.zeros(edge.shape, F32)
        cells = strip[...].astype(F32)
        cells = jnp.where(at_end, cells[:, side - 1], cells[:, 0])
        for part in range(2):
            at, first = part * (EDGE // 2), part * half_cols

            def corner(block):
                last = first + half_cols - 1
                low, high = block[REACH, first : first + 1], block[REACH, last : last + 1]
                return jnp.where(at_end, high, low)

            edge[at : at + 1] = corner(above)
            edge[at + 1 : at + half_rows + 1] = cells[:, part * lanes : (part + 1) * lanes]
            at += half_rows + 1
            edge[at : at + 1] = corner(below)
        target[tall * side : tall * side + EDGE] = edge[...].astype(BF16)


def fetch_kernel(*refs):
    count = len(refs) // 2
    sent = refs[-1]
    copies = [pltpu.make_async_copy(refs[i], refs[count + i], sent.at[i]) for i in range(count)]
    for copy in copies:
        copy.start()
    for copy in copies:
        copy.wait()


def fetch(*arrays):
    hbm, vmem = pl.BlockSpec(memory_space=pl.ANY), pl.BlockSpec(memory_space=pltpu.VMEM)
    return pl.pallas_call(
        fetch_kernel,
        out_shape=[pltpu.VMEM(array.shape, array.dtype) for array in arrays],
        in_specs=[hbm] * len(arrays),
        out_specs=[vmem] * len(arrays),
        scratch_shapes=[pltpu.SemaphoreType.DMA((len(arrays),))],
        compiler_params=pltpu.CompilerParams(vmem_limit_bytes=1 << 20),
    )(*[pltpu.with_memory_space_constraint(array, pltpu.HBM) for array in arrays])


def edge_columns(*arrays):
    vmem = pl.BlockSpec(memory_space=pltpu.VMEM)
    rows, side, lanes = arrays[2].shape
    shape = ((rows + 2 * REACH) * side + EDGE, lanes)
    return pl.pallas_call(
        columns_kernel,
        out_shape=(pltpu.VMEM(shape, BF16),) * 2,
        in_specs=[vmem] * 6,
        out_specs=(vmem,) * 2,
        scratch_shapes=[pltpu.VMEM((EDGE, lanes), F32)],
        compiler_params=pltpu.CompilerParams(vmem_limit_bytes=8 << 20),
    )(*resident(*arrays))


def scatter_sum(parts, axes):
    parts = lax.all_to_all(parts, axes, 0, 0, tiled=True)
    return parts.astype(F32).sum(axis=0).astype(BF16)


def gather(part, axes, count):
    parts = jnp.broadcast_to(part[None], (count,) + part.shape)
    return lax.all_to_all(parts, axes, 0, 0, tiled=True).reshape(-1, part.shape[1])


def per_device(images, first_kernel, projection, second_kernel, cotangent):
    image, upstream = images[0], cotangent[0]
    _, _, wide = upstream.shape
    _, _, lanes = image.shape
    rows_even, rows_odd, *strips = edges(image, upstream)
    rows_even, rows_odd = swap_neighbours(rows_even, rows_odd, GY, "gx_lo")
    packed = edge_columns(rows_even, rows_odd, *strips)
    cols_even, cols_odd = swap_neighbours(*packed, GX, "gy_hi")
    tile, *weights = fetch(image, first_kernel, projection, second_kernel)
    theirs = swap_pairs(upstream, "section")
    ring = [rows_even[REACH], rows_odd[REACH], cols_even[-EDGE:], cols_odd[-EDGE:]]
    ring = swap_pairs(jnp.concatenate(ring), "section")

    planes = lax.axis_size("section") * lax.axis_size("gy_hi") * lax.axis_size("gx_lo")
    lines = lax.axis_size("gx_hi")
    unit = 2 * planes * lines * 16
    total = -(-(9 * wide + 6 * lanes) // unit) * unit
    halo = (rows_even, rows_odd, cols_even, cols_odd)
    output, *kept = forward(tile, halo, *weights)
    output = swap_pairs(output, "section")
    chunk = total // 2 // planes if lines == 2 else 0
    mine, other = backward(theirs, ring, kept, *weights[1:], total, chunk)
    part = (mine.astype(F32) + swap_pairs(other, "core").astype(F32)).astype(BF16)
    part = scatter_sum(part.reshape(planes, -1, wide), PLANE)
    if lines == 2:
        pairs = [(0, 3), (1, 2), (2, 1), (3, 0)]
        theirs = lax.ppermute(part, GX, pairs)
        part = (part.astype(F32) + theirs.astype(F32)).astype(BF16)
    elif lines > 2:
        part = scatter_sum(part.reshape(lines, -1, wide), "gx_hi")
        part = gather(part, "gx_hi", lines)
    whole = gather(part, PLANE, planes)
    others = swap_pairs(whole, "core")
    shapes = (first_kernel.shape, projection.shape, second_kernel.shape)
    outs = tuple(jax.ShapeDtypeStruct(shape, F32) for shape in shapes)
    grads = unpack_call(unpack_own, chunk, (whole,), outs, {})
    outs = (jax.ShapeDtypeStruct(output.shape, BF16),) + outs
    output, *grads = unpack_call(
        unpack_other, chunk, (others, output, *grads), outs, {2: 1, 3: 2, 4: 3}
    )
    return (output[None], *grads)


def solution(mesh):
    shape = dict(mesh.shape)
    sizes = (shape["section"], shape["gy"] // 2, 2, shape["gx"] // 2, 2)
    names = ("section", "gy_hi", "core", "gx_hi", "gx_lo")
    split = jax.sharding.Mesh(mesh.devices.reshape(sizes), names)
    tiles = P("section", GY, GX, None)
    return jax.shard_map(
        per_device,
        mesh=split,
        in_specs=(tiles, P(), P(), P(), tiles),
        out_specs=(tiles, P(), P(), P()),
        check_vma=False,
    )
```

time: 228 us -> 73 us (0.32)
  waiting for transfers between devices: 153 us -> 18.6 us
  blocking collectives: 0 us -> 28.8 us
  starting transfers between devices: 31.2 us -> 11.8 us
  matrix products: 14.2 us -> 0 us
  between operations: 14.7 us -> 0.73 us
  Pallas kernels: 0 us -> 12.4 us
  local copies, waits for them, and re-layouts: 9.64 us -> 0.06 us
  other arithmetic: 4.38 us -> 0.34 us
    psum x1 -> x0, waiting for transfers between devices: 133 us -> none  [per_device(): lax.psum((grad_first, grad_projection, grad_second), ('section', 'gy', 'g...]
    all_to_all x0 -> x2, blocking collectives: none -> 28.8 us  [the longest x1 15.7 us: scatter_sum(): parts = lax.all_to_all(parts, axes, 0, 0, tiled=True)]
    ppermute x14 -> x10, starting transfers between devices: 31.1 us -> 11.8 us  [the longest x5 3.69 us: swap_pairs(): return lax.ppermute(block, axis, [(0, 1), (1, 0)])]
    dot_general x48 -> x0, matrix products: 14.2 us -> none  [the longest x18 5.6 us: conv_slopes(): jnp.einsum('pc,pd->cd', piece, slope, preferred_element_type=jnp.float32)]
    pallas_call x0 -> x7, Pallas kernels: none -> 12.4 us  [the longest x1 3.87 us: forward(): pl.pallas_call(forward_kernel, out_shape=(pltpu.VMEM((half_rows, half_col...]
    unnamed x20 -> x0, local copies, waits for them, and re-layouts: 7.35 us -> none
    ppermute x14 -> x10, waiting for transfers between devices: 20.6 us -> 18.6 us  [the longest x5 9.1 us: swap_pairs(): return lax.ppermute(block, axis, [(0, 1), (1, 0)])]
  transfers between devices with their start and end apart: 15 -> 10, of which waited for: 8 -> 6; matrix products, arithmetic and copies ran while one was open for 3% -> 0% of each run, Pallas kernels for 0% -> 9%
where the time goes in v3:
time: 73 us; the launch traced here: 72.7 us
  blocking collectives  28.8 us (39%)
  waiting for transfers between devices  18.6 us (25%)
  Pallas kernels  12.4 us (17%)
  starting transfers between devices  11.8 us (16%)
  between operations  0.73 us (1%)
    all_to_all x1, blocking collectives, scatter_sum(): parts = lax.all_to_all(parts, axes, 0, 0, tiled=True)  15.7 us
    all_to_all x1, blocking collectives, gather(): lax.all_to_all(parts, axes, 0, 0, tiled=True).reshape(-1, part.shape[1])  13.2 us
    ppermute x5, waiting for transfers between devices, swap_pairs(): return lax.ppermute(block, axis, [(0, 1), (1, 0)])  9.1 us
    ppermute x1, waiting for transfers between devices, per_device(): theirs = lax.ppermute(part, GX, pairs)  4.7 us
    pallas_call x1, Pallas kernels, forward(): pl.pallas_call(forward_kernel, out_shape=(pltpu.VMEM((half_rows, half_col...  3.87 us
    ppermute x5, starting transfers between devices, swap_pairs(): return lax.ppermute(block, axis, [(0, 1), (1, 0)])  3.69 us
    ppermute x2, starting transfers between devices, swap_neighbours(): odd = lax.ppermute(odd, names, both(far))  3.58 us
    pallas_call x1, Pallas kernels, backward(): pl.pallas_call(functools.partial(backward_kernel, chunk), out_shape=(pltp...  2.99 us
  transfers between devices with their start and end apart: 10, of which 6 were waited for; matrix products, arithmetic and copies ran while one was open for 0% of the time, Pallas kernels for 9%

profile of v3, /device:TPU:0, one launch (start us, length us, event | category | flops | bytes accessed | tf_op | source)
XLA Modules:
  0.0 72.7 jit_solution(10306848866759200088)
XLA Ops:
  0.6 1.2 %shard_map.84 = (bf16[6,64,128]{2,1,0:T(8,128)(2,1)S(1)}, bf16[6,64,128]{2,1,0:T(8,128)(2,1)S(1)}, bf16[32,8,128]{2,1,0:T(8,128)(2,1)S(1)}, bf16[32,8,128]{2,1,0...) custom-call(bf16[32,64,128]{2,1,0:T(8,128)(2,1)} %bitcast.12, ...), custom_call_target="tpu_custom_call" | custom-call | tf_op jit(solution)/shard_map/pallas_call | solution.py:405
  1.8 0.6 collective-permute-start.1
  2.4 2.6 %collective-permute-start.2 = (bf16[6,64,128]{2,1,0:T(8,128)(2,1)S(1)}, bf16[6,64,128]{2,1,0:T(8,128)(2,1)S(1)}, u32[]{:S(2)}, u32[]{:S(2)}) collective-permute-start(bf16[6,64,128]{2,1,0:T(8,128)(2,1)S(1)} %get-tuple-element.32), channel_id=1, source_target_pairs={{4,8},{8,4},{5,9},{9,5},{0,1},{1,0},{12,13},{13,12},{6,10},{10,6},... | collective-permute-start | bytes 294920 | tf_op jit(solution)/shard_map/ppermute | solution.py:364
  5.0 1.5 %collective-permute-start = (bf16[16,32,256]{2,1,0:T(8,128)(2,1)}, bf16[16,32,256]{2,1,0:T(8,128)(2,1)S(1)}, u32[]{:S(2)}, u32[]{:S(2)}) collective-permute-start(bf16[16,32,256]{2,1,0:T(8,128)(2,1)} %bitcast.15), channel_id=1, source_target_pairs={{0,16},{16,0},{1,17},{17,1},{2,18},{18,2},{3,19},{19,3},{4,20},{20... | collective-permute-start | bytes 786440 | tf_op jit(solution)/shard_map/ppermute | solution.py:344
  6.5 1.1 %collective-permute-done.2.rows_odd = bf16[6,64,128]{2,1,0:T(8,128)(2,1)S(1)} collective-permute-done((bf16[6,64,128]{2,1,0:T(8,128)(2,1)S(1)}, bf16[6,64,128]{2,1,0:T(8,128)(2,1)S(1)}, u32[]{:S(2)}, u32[]{:S(2)}) %collective-permute-start.2) | collective-permute-done | bytes 98336 | tf_op jit(solution)/shard_map/ppermute | solution.py:364
  7.7 2.1 %collective-permute-start.3 = (bf16[384,128]{1,0:T(8,128)(2,1)S(1)}, bf16[384,128]{1,0:T(8,128)(2,1)S(1)}, u32[]{:S(2)}, u32[]{:S(2)}) collective-permute-start(bf16[384,128]{1,0:T(8,128)(2,1)S(1)} %get-tuple-element.37), channel_id=1, source_target_pairs={{0,1},{1,0},{2,3},{3,2},{4,5},{5,4},{6,7},{7,6},{8,9},{9,8},{10,11... | collective-permute-start | bytes 294920 | tf_op jit(solution)/shard_map/ppermute | solution.py:365
  9.8 0.9 %collective-permute-start.4 = (bf16[384,128]{1,0:T(8,128)(2,1)S(1)}, bf16[384,128]{1,0:T(8,128)(2,1)S(1)}, u32[]{:S(2)}, u32[]{:S(2)}) collective-permute-start(bf16[384,128]{1,0:T(8,128)(2,1)S(1)} %get-tuple-element.38), channel_id=1, source_target_pairs={{1,2},{2,1},{9,10},{10,9},{0,8},{8,0},{3,11},{11,3},{5,6},{6,5},{1... | collective-permute-start | bytes 294920 | tf_op jit(solution)/shard_map/ppermute | solution.py:364
  10.7 2.2 %collective-permute-done.3.cols_even = bf16[384,128]{1,0:T(8,128)(2,1)S(1)} collective-permute-done((bf16[384,128]{1,0:T(8,128)(2,1)S(1)}, bf16[384,128]{1,0:T(8,128)(2,1)S(1)}, u32[]{:S(2)}, u32[]{:S(2)}) %collective-permute-start.3) | collective-permute-done | bytes 98336 | tf_op jit(solution)/shard_map/ppermute | solution.py:365
  12.9 1.5 %collective-permute-done.4.cols_odd = bf16[384,128]{1,0:T(8,128)(2,1)S(1)} collective-permute-done((bf16[384,128]{1,0:T(8,128)(2,1)S(1)}, bf16[384,128]{1,0:T(8,128)(2,1)S(1)}, u32[]{:S(2)}, u32[]{:S(2)}) %collective-permute-start.4) | collective-permute-done | bytes 98336 | tf_op jit(solution)/shard_map/ppermute | solution.py:364
  14.4 1.6 %collective-permute-start.5 = (bf16[224,128]{1,0:T(8,128)(2,1)S(1)}, bf16[224,128]{1,0:T(8,128)(2,1)S(1)}, u32[]{:S(2)}, u32[]{:S(2)}) collective-permute-start(bf16[224,128]{1,0:T(8,128)(2,1)S(1)} %pad_maximum_fusion), channel_id=1, source_target_pairs={{0,16},{16,0},{1,17},{17,1},{2,18},{18,2},{3,19},{19,3},{4,20},{20... | collective-permute-start | bytes 172040 | tf_op jit(solution)/shard_map/ppermute | solution.py:344
  16.0 1.6 %shard_map.86 = (bf16[32,64,128]{2,1,0:T(8,128)(2,1)S(1)}, bf16[3,3,128,128]{3,2,1,0:T(8,128)(2,1)S(1)}, bf16[128,256]{1,0:T(8,128)(2,1)S(1)}, bf16[3,3,256,256]{3,2,1,0:T(8,128)(2,1)S(1)}) custom-call(bf16[32,64,128]{2,1,0:T(8,128)(2,1)} %bitcast.13, bf16[3,3,128,128]{3,2,1,0:T(8,128)(2,1)} %refs_1_.1, bf16[128,256]{1,0:T(8,128)(2,1)} %refs_2_.1, ...), custom_call_target="tpu_custom_call" | custom-call | tf_op jit(solution)/shard_map/pallas_call | solution.py:464
  17.6 3.9 %shard_map.87 = (bf16[16,32,256]{2,1,0:T(8,128)(2,1)S(1)}, bf16[42,80,384]{2,1,0:T(8,128)(2,1)S(1)}, f32[20,80,256]{2,1,0:T(8,128)S(1)}, bf16[20,48,768]{2,1,0:T...) custom-call(bf16[32,64,128]{2,1,0:T(8,128)(2,1)S(1)} %get-tuple-element.39.tile, ...), custom_call_target="tpu_custom_call" | custom-call | tf_op jit(solution)/shard_map/pallas_call | solution.py:223
  21.5 3.0 %shard_map.88 = (bf16[1536,256]{1,0:T(8,128)(2,1)S(1)}, bf16[1536,256]{1,0:T(8,128)(2,1)S(1)}) custom-call(bf16[16,32,256]{2,1,0:T(8,128)(2,1)S(1)} %collective-permute-done.theirs, bf16[224,128]{1,0:T(8,128)(2,1)S(1)} %collective-permute-done.5.ring, bf16[42,80,384]{2,1,0:T(8,128)(2,1)S(1)} %get-tuple-element.43.taps_one, ...), custom_call_target="tpu_custom_call" | custom-call | tf_op jit(solution)/shard_map/pallas_call | solution.py:250
  24.5 2.3 %collective-permute-done.6 = bf16[1536,256]{1,0:T(8,128)(2,1)S(1)} collective-permute-done((bf16[1536,256]{1,0:T(8,128)(2,1)S(1)}, bf16[1536,256]{1,0:T(8,128)(2,1)S(1)}, u32[]{:S(2)}, u32[]{:S(2)}) %collective-permute-start.6) | collective-permute-done | bytes 786464 | tf_op jit(solution)/shard_map/ppermute | solution.py:344
  26.8 0.2 add_convert_fusion
  27.0 15.7 %all_to_all.10 = bf16[8,192,256]{2,1,0:T(8,128)(2,1)S(1)} all-to-all(bf16[8,192,256]{2,1,0:T(8,128)(2,1)S(1)} %bitcast.11), channel_id=1, replica_groups=mesh['section'=2,'gy_hi'=2,'core'=2,'gx_hi'=2,'gx_lo'=2] {'section','gy_..., dimensions={0} | all-to-all | bytes 1572864 | tf_op jit(solution)/shard_map/all_to_all | solution.py:489
  42.7 0.1 reduce_sum.12
  42.8 1.9 %collective-permute-start.7 = (bf16[192,256]{1,0:T(8,128)(2,1)S(1)}, bf16[192,256]{1,0:T(8,128)(2,1)S(1)}, u32[]{:S(2)}, u32[]{:S(2)}) collective-permute-start(bf16[192,256]{1,0:T(8,128)(2,1)S(1)} %reduce_sum.12), channel_id=1, source_target_pairs={{0,3},{1,2},{2,1},{3,0},{4,7},{5,6},{6,5},{7,4},{8,11},{9,10},{10,... | collective-permute-start | bytes 294920 | tf_op jit(solution)/shard_map/ppermute | solution.py:524
  44.7 4.7 %collective-permute-done.7 = bf16[192,256]{1,0:T(8,128)(2,1)S(1)} collective-permute-done((bf16[192,256]{1,0:T(8,128)(2,1)S(1)}, bf16[192,256]{1,0:T(8,128)(2,1)S(1)}, u32[]{:S(2)}, u32[]{:S(2)}) %collective-permute-start.7) | collective-permute-done | bytes 98336 | tf_op jit(solution)/shard_map/ppermute | solution.py:524
  49.5 13.2 %all_to_all.11 = bf16[8,192,256]{2,1,0:T(8,128)(2,1)S(1)} all-to-all(bf16[8,192,256]{2,1,0:T(8,128)(2,1)S(1)} %broadcast_in_dim.4), channel_id=1, replica_groups=mesh['section'=2,'gy_hi'=2,'core'=2,'gx_hi'=2,'gx_lo'=2] {'section','gy_..., dimensions={0} | all-to-all | bytes 1572864 | tf_op jit(solution)/shard_map/all_to_all | solution.py:495
  62.7 0.6 collective-permute-start.9
  63.2 1.3 %shard_map.89 = (f32[3,3,128,128]{3,2,1,0:T(8,128)}, f32[128,256]{1,0:T(8,128)}, f32[3,3,256,256]{3,2,1,0:T(8,128)}) custom-call(bf16[1536,256]{1,0:T(8,128)(2,1)S(1)} %bitcast.10), custom_call_target="tpu_custom_call" | custom-call | tf_op jit(solution)/shard_map/pallas_call | solution.py:329
  64.6 6.8 %collective-permute-done.9.features = bf16[16,32,256]{2,1,0:T(8,128)(2,1)S(1)} collective-permute-done((bf16[16,32,256]{2,1,0:T(8,128)(2,1)S(1)}, bf16[16,32,256]{2,1,0:T(8,128)(2,1)S(1)}, u32[]{:S(2)}, u32[]{:S(2)}) %collective-permute-start.9) | collective-permute-done | bytes 262176 | tf_op jit(solution)/shard_map/ppermute | solution.py:344
  71.4 1.4 %shard_map.90 = (bf16[16,32,256]{2,1,0:T(8,128)(2,1)}, f32[3,3,128,128]{3,2,1,0:T(8,128)}, f32[128,256]{1,0:T(8,128)}, f32[3,3,256,256]{3,2,1,0:T(8,128)}) custom-call(bf16[1536,256]{1,0:T(8,128)(2,1)S(1)} %collective-permute-done.8.source, ...), custom_call_target="tpu_custom_call", output_to_operand_aliasing={{1}: (2, {}), {2}: (3, {}), {3}: (4, {})} | custom-call | tf_op jit(solution)/shard_map/pallas_call | solution.py:329
  (14 shorter events, 0.3 us)
Async XLA Ops:
  1.8 4.7 %collective-permute-start.1 = (bf16[6,64,128]{2,1,0:T(8,128)(2,1)S(1)}, bf16[6,64,128]{2,1,0:T(8,128)(2,1)S(1)}, u32[]{:S(2)}, u32[]{:S(2)}) collective-permute-start(bf16[6,64,128]{2,1,0:T(8,128)(2,1)S(1)} %get-tuple-element.31), channel_id=1, source_target_pairs={{0,4},{4,0},{8,12},{12,8},{1,5},{5,1},{9,13},{13,9},{2,6},{6,2},{1... | collective-permute-start | bytes 294920 | tf_op jit(solution)/shard_map/ppermute | solution.py:365
  2.4 5.2 %collective-permute-start.2 = (bf16[6,64,128]{2,1,0:T(8,128)(2,1)S(1)}, bf16[6,64,128]{2,1,0:T(8,128)(2,1)S(1)}, u32[]{:S(2)}, u32[]{:S(2)}) collective-permute-start(bf16[6,64,128]{2,1,0:T(8,128)(2,1)S(1)} %get-tuple-element.32), channel_id=1, source_target_pairs={{4,8},{8,4},{5,9},{9,5},{0,1},{1,0},{12,13},{13,12},{6,10},{10,6},... | collective-permute-start | bytes 294920 | tf_op jit(solution)/shard_map/ppermute | solution.py:364
  5.0 16.4 %collective-permute-start = (bf16[16,32,256]{2,1,0:T(8,128)(2,1)}, bf16[16,32,256]{2,1,0:T(8,128)(2,1)S(1)}, u32[]{:S(2)}, u32[]{:S(2)}) collective-permute-start(bf16[16,32,256]{2,1,0:T(8,128)(2,1)} %bitcast.15), channel_id=1, source_target_pairs={{0,16},{16,0},{1,17},{17,1},{2,18},{18,2},{3,19},{19,3},{4,20},{20... | collective-permute-start | bytes 786440 | tf_op jit(solution)/shard_map/ppermute | solution.py:344
  7.7 5.2 %collective-permute-start.3 = (bf16[384,128]{1,0:T(8,128)(2,1)S(1)}, bf16[384,128]{1,0:T(8,128)(2,1)S(1)}, u32[]{:S(2)}, u32[]{:S(2)}) collective-permute-start(bf16[384,128]{1,0:T(8,128)(2,1)S(1)} %get-tuple-element.37), channel_id=1, source_target_pairs={{0,1},{1,0},{2,3},{3,2},{4,5},{5,4},{6,7},{7,6},{8,9},{9,8},{10,11... | collective-permute-start | bytes 294920 | tf_op jit(solution)/shard_map/ppermute | solution.py:365
  9.8 4.6 %collective-permute-start.4 = (bf16[384,128]{1,0:T(8,128)(2,1)S(1)}, bf16[384,128]{1,0:T(8,128)(2,1)S(1)}, u32[]{:S(2)}, u32[]{:S(2)}) collective-permute-start(bf16[384,128]{1,0:T(8,128)(2,1)S(1)} %get-tuple-element.38), channel_id=1, source_target_pairs={{1,2},{2,1},{9,10},{10,9},{0,8},{8,0},{3,11},{11,3},{5,6},{6,5},{1... | collective-permute-start | bytes 294920 | tf_op jit(solution)/shard_map/ppermute | solution.py:364
  14.4 7.0 %collective-permute-start.5 = (bf16[224,128]{1,0:T(8,128)(2,1)S(1)}, bf16[224,128]{1,0:T(8,128)(2,1)S(1)}, u32[]{:S(2)}, u32[]{:S(2)}) collective-permute-start(bf16[224,128]{1,0:T(8,128)(2,1)S(1)} %pad_maximum_fusion), channel_id=1, source_target_pairs={{0,16},{16,0},{1,17},{17,1},{2,18},{18,2},{3,19},{19,3},{4,20},{20... | collective-permute-start | bytes 172040 | tf_op jit(solution)/shard_map/ppermute | solution.py:344
  24.5 2.4 %collective-permute-start.6 = (bf16[1536,256]{1,0:T(8,128)(2,1)S(1)}, bf16[1536,256]{1,0:T(8,128)(2,1)S(1)}, u32[]{:S(2)}, u32[]{:S(2)}) collective-permute-start(bf16[1536,256]{1,0:T(8,128)(2,1)S(1)} %get-tuple-element.49), channel_id=1, source_target_pairs={{0,4},{4,0},{1,5},{5,1},{2,6},{6,2},{3,7},{7,3},{8,12},{12,8},{9,1... | collective-permute-start | bytes 2359304 | tf_op jit(solution)/shard_map/ppermute | solution.py:344
  42.8 6.6 %collective-permute-start.7 = (bf16[192,256]{1,0:T(8,128)(2,1)S(1)}, bf16[192,256]{1,0:T(8,128)(2,1)S(1)}, u32[]{:S(2)}, u32[]{:S(2)}) collective-permute-start(bf16[192,256]{1,0:T(8,128)(2,1)S(1)} %reduce_sum.12), channel_id=1, source_target_pairs={{0,3},{1,2},{2,1},{3,0},{4,7},{5,6},{6,5},{7,4},{8,11},{9,10},{10,... | collective-permute-start | bytes 294920 | tf_op jit(solution)/shard_map/ppermute | solution.py:524
  62.7 8.7 %collective-permute-start.8 = (bf16[1536,256]{1,0:T(8,128)(2,1)S(1)}, bf16[1536,256]{1,0:T(8,128)(2,1)S(1)}, u32[]{:S(2)}, u32[]{:S(2)}) collective-permute-start(bf16[1536,256]{1,0:T(8,128)(2,1)S(1)} %bitcast.9), channel_id=1, source_target_pairs={{0,4},{4,0},{1,5},{5,1},{2,6},{6,2},{3,7},{7,3},{8,12},{12,8},{9,1... | collective-permute-start | bytes 2359304 | tf_op jit(solution)/shard_map/ppermute | solution.py:344
  62.7 8.7 %collective-permute-start.9 = (bf16[16,32,256]{2,1,0:T(8,128)(2,1)S(1)}, bf16[16,32,256]{2,1,0:T(8,128)(2,1)S(1)}, u32[]{:S(2)}, u32[]{:S(2)}) collective-permute-start(bf16[16,32,256]{2,1,0:T(8,128)(2,1)S(1)} %get-tuple-element.50), channel_id=1, source_target_pairs={{0,16},{16,0},{1,17},{17,1},{2,18},{18,2},{3,19},{19,3},{4,20},{20... | collective-permute-start | bytes 786440 | tf_op jit(solution)/shard_map/ppermute | solution.py:344

commit v4 on v3

--- a/solution.py
+++ b/solution.py
@@ -101,9 +101,8 @@
     left = jnp.where(gx == 0, half_pitch, half_cols + SIDE // 2)
     keep = (row >= low) & (row < high) & ((col < right) | (col >= left))
     middle = jnp.where(keep, middle, 0.0)
-    middle = jnp.concatenate([middle, middle[:, half_pitch - 8 :]], axis=1)
     spread_taps(middle, taps_mid, wide)
-    pitch_two = half_pitch + 8
+    pitch_two = half_pitch
     outs = half_rows + 2
     part = outs
 
@@ -218,7 +217,7 @@
     rows, cols, lanes = tile.shape
     half_rows, half_cols, wide = rows // 2, cols // 2, projection.shape[1]
     pitch = cols + 2 * SIDE
-    pitch_two = pitch // 2 + 8
+    pitch_two = pitch // 2
     vmem = pl.BlockSpec(memory_space=pltpu.VMEM)
     return pl.pallas_call(
         forward_kernel,
@@ -366,12 +365,10 @@
     return even, odd
 
 
-def edges_kernel(
-    image, upstream, rows_even, rows_odd, tile_even, tile_odd, strip_even, strip_odd, sent,
-):
-    rows, cols, lanes = image.shape
+def rows_kernel(image, upstream, rows_even, rows_odd, sent):
+    rows, _, lanes = image.shape
     half_rows, half_cols, _ = upstream.shape
-    lower, left = lax.axis_index("core") == 0, lax.axis_index("gx_lo") == 0
+    lower = lax.axis_index("core") == 0
     copies = []
 
     def send(source, target):
@@ -388,6 +385,21 @@
                 upstream.at[row, :, part * lanes : (part + 1) * lanes],
                 target.at[REACH, part * half_cols : (part + 1) * half_cols],
             )
+    for copy in copies:
+        copy.wait()
+
+
+def strips_kernel(image, upstream, tile_even, tile_odd, strip_even, strip_odd, sent):
+    _, cols, _ = image.shape
+    _, half_cols, _ = upstream.shape
+    left = lax.axis_index("gx_lo") == 0
+    copies = []
+
+    def send(source, target):
+        copy = pltpu.make_async_copy(source, target, sent.at[len(copies)])
+        copy.start()
+        copies.append(copy)
+
     for target, strip, at_end in ((tile_odd, strip_odd, ~left), (tile_even, strip_even, left)):
         start = pl.multiple_of(jnp.where(at_end, cols - SIDE, 0), SIDE)
         cell = pl.multiple_of(jnp.where(at_end, half_cols - SIDE, 0), SIDE)
@@ -397,17 +409,14 @@
         copy.wait()
 
 
-def edges(image, upstream):
+def cut(kernel, shapes, image, upstream):
     hbm, vmem = pl.BlockSpec(memory_space=pl.ANY), pl.BlockSpec(memory_space=pltpu.VMEM)
-    rows, cols, lanes = image.shape
-    half_rows, _, wide = upstream.shape
-    shapes = [(REACH + 1, cols, lanes), (rows, SIDE, lanes), (half_rows, SIDE, wide)]
     return pl.pallas_call(
-        edges_kernel,
+        kernel,
         out_shape=[pltpu.VMEM(shape, BF16) for shape in shapes for _ in range(2)],
         in_specs=[hbm, hbm],
-        out_specs=[vmem] * 6,
-        scratch_shapes=[pltpu.SemaphoreType.DMA((10,))],
+        out_specs=[vmem] * (2 * len(shapes)),
+        scratch_shapes=[pltpu.SemaphoreType.DMA((6,))],
         compiler_params=pltpu.CompilerParams(vmem_limit_bytes=4 << 20),
     )(*[pltpu.with_memory_space_constraint(array, pltpu.HBM) for array in (image, upstream)])
 
@@ -497,9 +506,11 @@
 
 def per_device(images, first_kernel, projection, second_kernel, cotangent):
     image, upstream = images[0], cotangent[0]
-    _, _, wide = upstream.shape
-    _, _, lanes = image.shape
-    rows_even, rows_odd, *strips = edges(image, upstream)
+    half_rows, _, wide = upstream.shape
+    rows, cols, lanes = image.shape
+    rows_even, rows_odd = cut(rows_kernel, [(REACH + 1, cols, lanes)], image, upstream)
+    shapes = [(rows, SIDE, lanes), (half_rows, SIDE, wide)]
+    strips = cut(strips_kernel, shapes, image, upstream)
     rows_even, rows_odd = swap_neighbours(rows_even, rows_odd, GY, "gx_lo")
     packed = edge_columns(rows_even, rows_odd, *strips)
     cols_even, cols_odd = swap_neighbours(*packed, GX, "gy_hi")

time: 73 us -> 72.7 us (level)
  waiting for transfers between devices: 18.6 us -> 17.6 us
    ppermute x2, waiting for transfers between devices: 2.6 us -> 1.6 us  [swap_neighbours(): odd = lax.ppermute(odd, names, both(far))]
    pallas_call x1 -> x2, Pallas kernels: 1.18 us -> 2.02 us  [cut(): pl.pallas_call(kernel, out_shape=[pltpu.VMEM(shape, BF16) for shape in sh...]
  transfers between devices with their start and end apart: 10 -> 10, of which waited for: 6 -> 6; matrix products, arithmetic and copies ran while one was open for 0% -> 0% of each run, Pallas kernels for 9% -> 11%
where the time goes in v4:
time: 72.7 us; the launch traced here: 72.4 us
  blocking collectives  28.8 us (40%)
  waiting for transfers between devices  17.6 us (24%)
  Pallas kernels  13 us (18%)
  starting transfers between devices  11.8 us (16%)
  between operations  0.74 us (1%)
    all_to_all x1, blocking collectives, scatter_sum(): parts = lax.all_to_all(parts, axes, 0, 0, tiled=True)  15.7 us
    all_to_all x1, blocking collectives, gather(): lax.all_to_all(parts, axes, 0, 0, tiled=True).reshape(-1, part.shape[1])  13.2 us
    ppermute x5, waiting for transfers between devices, swap_pairs(): return lax.ppermute(block, axis, [(0, 1), (1, 0)])  9.1 us
    ppermute x1, waiting for transfers between devices, per_device(): theirs = lax.ppermute(part, GX, pairs)  4.7 us
    ppermute x5, starting transfers between devices, swap_pairs(): return lax.ppermute(block, axis, [(0, 1), (1, 0)])  3.69 us
    pallas_call x1, Pallas kernels, forward(): pl.pallas_call(forward_kernel, out_shape=(pltpu.VMEM((half_rows, half_col...  3.67 us
    ppermute x2, starting transfers between devices, swap_neighbours(): odd = lax.ppermute(odd, names, both(far))  3.58 us
    pallas_call x1, Pallas kernels, backward(): pl.pallas_call(functools.partial(backward_kernel, chunk), out_shape=(pltp...  2.98 us
  transfers between devices with their start and end apart: 10, of which 6 were waited for; matrix products, arithmetic and copies ran while one was open for 0% of the time, Pallas kernels for 11%

profile of v4, /device:TPU:0, one launch (start us, length us, event | category | flops | bytes accessed | tf_op | source)
XLA Modules:
  0.0 72.4 jit_solution(15721778552342819833)
XLA Ops:
  0.6 1.0 %shard_map.84 = (bf16[6,64,128]{2,1,0:T(8,128)(2,1)S(1)}, bf16[6,64,128]{2,1,0:T(8,128)(2,1)S(1)}) custom-call(bf16[32,64,128]{2,1,0:T(8,128)(2,1)} %bitcast.11, bf16[16,32,256]{2,1,0:T(8,128)(2,1)} %bitcast.15), custom_call_target="tpu_custom_call" | custom-call | tf_op jit(solution)/shard_map/pallas_call | solution.py:414
  1.7 0.6 collective-permute-start.1
  2.2 2.6 %collective-permute-start.2 = (bf16[6,64,128]{2,1,0:T(8,128)(2,1)S(1)}, bf16[6,64,128]{2,1,0:T(8,128)(2,1)S(1)}, u32[]{:S(2)}, u32[]{:S(2)}) collective-permute-start(bf16[6,64,128]{2,1,0:T(8,128)(2,1)S(1)} %get-tuple-element.32), channel_id=1, source_target_pairs={{4,8},{8,4},{5,9},{9,5},{0,1},{1,0},{12,13},{13,12},{6,10},{10,6},... | collective-permute-start | bytes 294920 | tf_op jit(solution)/shard_map/ppermute | solution.py:363
  4.9 1.5 %collective-permute-start = (bf16[16,32,256]{2,1,0:T(8,128)(2,1)}, bf16[16,32,256]{2,1,0:T(8,128)(2,1)S(1)}, u32[]{:S(2)}, u32[]{:S(2)}) collective-permute-start(bf16[16,32,256]{2,1,0:T(8,128)(2,1)} %bitcast.16), channel_id=1, source_target_pairs={{0,16},{16,0},{1,17},{17,1},{2,18},{18,2},{3,19},{19,3},{4,20},{20... | collective-permute-start | bytes 786440 | tf_op jit(solution)/shard_map/ppermute | solution.py:343
  6.4 1.0 %shard_map.85 = (bf16[32,8,128]{2,1,0:T(8,128)(2,1)S(1)}, bf16[32,8,128]{2,1,0:T(8,128)(2,1)S(1)}, bf16[16,8,256]{2,1,0:T(8,128)(2,1)S(1)}, bf16[16,8,256]{2,1,0:T(8,128)(2,1)S(1)}) custom-call(bf16[32,64,128]{2,1,0:T(8,128)(2,1)} %bitcast.12, bf16[16,32,256]{2,1,0:T(8,128)(2,1)} %bitcast.17), custom_call_target="tpu_custom_call" | custom-call | tf_op jit(solution)/shard_map/pallas_call | solution.py:414
  7.6 2.1 %collective-permute-start.3 = (bf16[384,128]{1,0:T(8,128)(2,1)S(1)}, bf16[384,128]{1,0:T(8,128)(2,1)S(1)}, u32[]{:S(2)}, u32[]{:S(2)}) collective-permute-start(bf16[384,128]{1,0:T(8,128)(2,1)S(1)} %get-tuple-element.37), channel_id=1, source_target_pairs={{0,1},{1,0},{2,3},{3,2},{4,5},{5,4},{6,7},{7,6},{8,9},{9,8},{10,11... | collective-permute-start | bytes 294920 | tf_op jit(solution)/shard_map/ppermute | solution.py:364
  9.6 0.9 %collective-permute-start.4 = (bf16[384,128]{1,0:T(8,128)(2,1)S(1)}, bf16[384,128]{1,0:T(8,128)(2,1)S(1)}, u32[]{:S(2)}, u32[]{:S(2)}) collective-permute-start(bf16[384,128]{1,0:T(8,128)(2,1)S(1)} %get-tuple-element.38), channel_id=1, source_target_pairs={{1,2},{2,1},{9,10},{10,9},{0,8},{8,0},{3,11},{11,3},{5,6},{6,5},{1... | collective-permute-start | bytes 294920 | tf_op jit(solution)/shard_map/ppermute | solution.py:363
  10.6 2.2 %collective-permute-done.3.cols_even = bf16[384,128]{1,0:T(8,128)(2,1)S(1)} collective-permute-done((bf16[384,128]{1,0:T(8,128)(2,1)S(1)}, bf16[384,128]{1,0:T(8,128)(2,1)S(1)}, u32[]{:S(2)}, u32[]{:S(2)}) %collective-permute-start.3) | collective-permute-done | bytes 98336 | tf_op jit(solution)/shard_map/ppermute | solution.py:364
  12.8 1.5 %collective-permute-done.4.cols_odd = bf16[384,128]{1,0:T(8,128)(2,1)S(1)} collective-permute-done((bf16[384,128]{1,0:T(8,128)(2,1)S(1)}, bf16[384,128]{1,0:T(8,128)(2,1)S(1)}, u32[]{:S(2)}, u32[]{:S(2)}) %collective-permute-start.4) | collective-permute-done | bytes 98336 | tf_op jit(solution)/shard_map/ppermute | solution.py:363
  14.3 1.6 %collective-permute-start.5 = (bf16[224,128]{1,0:T(8,128)(2,1)S(1)}, bf16[224,128]{1,0:T(8,128)(2,1)S(1)}, u32[]{:S(2)}, u32[]{:S(2)}) collective-permute-start(bf16[224,128]{1,0:T(8,128)(2,1)S(1)} %pad_maximum_fusion), channel_id=1, source_target_pairs={{0,16},{16,0},{1,17},{17,1},{2,18},{18,2},{3,19},{19,3},{4,20},{20... | collective-permute-start | bytes 172040 | tf_op jit(solution)/shard_map/ppermute | solution.py:343
  15.8 1.6 %shard_map.87 = (bf16[32,64,128]{2,1,0:T(8,128)(2,1)S(1)}, bf16[3,3,128,128]{3,2,1,0:T(8,128)(2,1)S(1)}, bf16[128,256]{1,0:T(8,128)(2,1)S(1)}, bf16[3,3,256,256]{3,2,1,0:T(8,128)(2,1)S(1)}) custom-call(bf16[32,64,128]{2,1,0:T(8,128)(2,1)} %bitcast.13, bf16[3,3,128,128]{3,2,1,0:T(8,128)(2,1)} %refs_1_.1, bf16[128,256]{1,0:T(8,128)(2,1)} %refs_2_.1, ...), custom_call_target="tpu_custom_call" | custom-call | tf_op jit(solution)/shard_map/pallas_call | solution.py:473
  17.4 3.7 %shard_map.88 = (bf16[16,32,256]{2,1,0:T(8,128)(2,1)S(1)}, bf16[42,80,384]{2,1,0:T(8,128)(2,1)S(1)}, f32[20,80,256]{2,1,0:T(8,128)S(1)}, bf16[20,40,768]{2,1,0:T...) custom-call(bf16[32,64,128]{2,1,0:T(8,128)(2,1)S(1)} %get-tuple-element.39.tile, ...), custom_call_target="tpu_custom_call" | custom-call | tf_op jit(solution)/shard_map/pallas_call | solution.py:222
  21.1 3.0 %shard_map.89 = (bf16[1536,256]{1,0:T(8,128)(2,1)S(1)}, bf16[1536,256]{1,0:T(8,128)(2,1)S(1)}) custom-call(bf16[16,32,256]{2,1,0:T(8,128)(2,1)S(1)} %collective-permute-done.theirs, bf16[224,128]{1,0:T(8,128)(2,1)S(1)} %collective-permute-done.5.ring, bf16[42,80,384]{2,1,0:T(8,128)(2,1)S(1)} %get-tuple-element.43.taps_one, ...), custom_call_target="tpu_custom_call" | custom-call | tf_op jit(solution)/shard_map/pallas_call | solution.py:249
  24.2 2.3 %collective-permute-done.6 = bf16[1536,256]{1,0:T(8,128)(2,1)S(1)} collective-permute-done((bf16[1536,256]{1,0:T(8,128)(2,1)S(1)}, bf16[1536,256]{1,0:T(8,128)(2,1)S(1)}, u32[]{:S(2)}, u32[]{:S(2)}) %collective-permute-start.6) | collective-permute-done | bytes 786464 | tf_op jit(solution)/shard_map/ppermute | solution.py:343
  26.5 0.2 add_convert_fusion
  26.7 15.7 %all_to_all.10 = bf16[8,192,256]{2,1,0:T(8,128)(2,1)S(1)} all-to-all(bf16[8,192,256]{2,1,0:T(8,128)(2,1)S(1)} %bitcast.14), channel_id=1, replica_groups=mesh['section'=2,'gy_hi'=2,'core'=2,'gx_hi'=2,'gx_lo'=2] {'section','gy_..., dimensions={0} | all-to-all | bytes 1572864 | tf_op jit(solution)/shard_map/all_to_all | solution.py:498
  42.3 0.1 reduce_sum.12
  42.4 1.9 %collective-permute-start.7 = (bf16[192,256]{1,0:T(8,128)(2,1)S(1)}, bf16[192,256]{1,0:T(8,128)(2,1)S(1)}, u32[]{:S(2)}, u32[]{:S(2)}) collective-permute-start(bf16[192,256]{1,0:T(8,128)(2,1)S(1)} %reduce_sum.12), channel_id=1, source_target_pairs={{0,3},{1,2},{2,1},{3,0},{4,7},{5,6},{6,5},{7,4},{8,11},{9,10},{10,... | collective-permute-start | bytes 294920 | tf_op jit(solution)/shard_map/ppermute | solution.py:535
  44.3 4.7 %collective-permute-done.7 = bf16[192,256]{1,0:T(8,128)(2,1)S(1)} collective-permute-done((bf16[192,256]{1,0:T(8,128)(2,1)S(1)}, bf16[192,256]{1,0:T(8,128)(2,1)S(1)}, u32[]{:S(2)}, u32[]{:S(2)}) %collective-permute-start.7) | collective-permute-done | bytes 98336 | tf_op jit(solution)/shard_map/ppermute | solution.py:535
  49.1 13.2 %all_to_all.11 = bf16[8,192,256]{2,1,0:T(8,128)(2,1)S(1)} all-to-all(bf16[8,192,256]{2,1,0:T(8,128)(2,1)S(1)} %broadcast_in_dim.4), channel_id=1, replica_groups=mesh['section'=2,'gy_hi'=2,'core'=2,'gx_hi'=2,'gx_lo'=2] {'section','gy_..., dimensions={0} | all-to-all | bytes 1572864 | tf_op jit(solution)/shard_map/all_to_all | solution.py:504
  62.3 0.6 collective-permute-start.9
  62.9 1.3 %shard_map.90 = (f32[3,3,128,128]{3,2,1,0:T(8,128)}, f32[128,256]{1,0:T(8,128)}, f32[3,3,256,256]{3,2,1,0:T(8,128)}) custom-call(bf16[1536,256]{1,0:T(8,128)(2,1)S(1)} %bitcast.10), custom_call_target="tpu_custom_call" | custom-call | tf_op jit(solution)/shard_map/pallas_call | solution.py:328
  64.2 6.8 %collective-permute-done.9.features = bf16[16,32,256]{2,1,0:T(8,128)(2,1)S(1)} collective-permute-done((bf16[16,32,256]{2,1,0:T(8,128)(2,1)S(1)}, bf16[16,32,256]{2,1,0:T(8,128)(2,1)S(1)}, u32[]{:S(2)}, u32[]{:S(2)}) %collective-permute-start.9) | collective-permute-done | bytes 262176 | tf_op jit(solution)/shard_map/ppermute | solution.py:343
  71.0 1.4 %shard_map.91 = (bf16[16,32,256]{2,1,0:T(8,128)(2,1)}, f32[3,3,128,128]{3,2,1,0:T(8,128)}, f32[128,256]{1,0:T(8,128)}, f32[3,3,256,256]{3,2,1,0:T(8,128)}) custom-call(bf16[1536,256]{1,0:T(8,128)(2,1)S(1)} %collective-permute-done.8.source, ...), custom_call_target="tpu_custom_call", output_to_operand_aliasing={{1}: (2, {}), {2}: (3, {}), {3}: (4, {})} | custom-call | tf_op jit(solution)/shard_map/pallas_call | solution.py:328
  (15 shorter events, 0.4 us)
Async XLA Ops:
  1.7 5.7 %collective-permute-start.1 = (bf16[6,64,128]{2,1,0:T(8,128)(2,1)S(1)}, bf16[6,64,128]{2,1,0:T(8,128)(2,1)S(1)}, u32[]{:S(2)}, u32[]{:S(2)}) collective-permute-start(bf16[6,64,128]{2,1,0:T(8,128)(2,1)S(1)} %get-tuple-element.31), channel_id=1, source_target_pairs={{0,4},{4,0},{8,12},{12,8},{1,5},{5,1},{9,13},{13,9},{2,6},{6,2},{1... | collective-permute-start | bytes 294920 | tf_op jit(solution)/shard_map/ppermute | solution.py:364
  2.2 5.2 %collective-permute-start.2 = (bf16[6,64,128]{2,1,0:T(8,128)(2,1)S(1)}, bf16[6,64,128]{2,1,0:T(8,128)(2,1)S(1)}, u32[]{:S(2)}, u32[]{:S(2)}) collective-permute-start(bf16[6,64,128]{2,1,0:T(8,128)(2,1)S(1)} %get-tuple-element.32), channel_id=1, source_target_pairs={{4,8},{8,4},{5,9},{9,5},{0,1},{1,0},{12,13},{13,12},{6,10},{10,6},... | collective-permute-start | bytes 294920 | tf_op jit(solution)/shard_map/ppermute | solution.py:363
  4.9 16.2 %collective-permute-start = (bf16[16,32,256]{2,1,0:T(8,128)(2,1)}, bf16[16,32,256]{2,1,0:T(8,128)(2,1)S(1)}, u32[]{:S(2)}, u32[]{:S(2)}) collective-permute-start(bf16[16,32,256]{2,1,0:T(8,128)(2,1)} %bitcast.16), channel_id=1, source_target_pairs={{0,16},{16,0},{1,17},{17,1},{2,18},{18,2},{3,19},{19,3},{4,20},{20... | collective-permute-start | bytes 786440 | tf_op jit(solution)/shard_map/ppermute | solution.py:343
  7.6 5.2 %collective-permute-start.3 = (bf16[384,128]{1,0:T(8,128)(2,1)S(1)}, bf16[384,128]{1,0:T(8,128)(2,1)S(1)}, u32[]{:S(2)}, u32[]{:S(2)}) collective-permute-start(bf16[384,128]{1,0:T(8,128)(2,1)S(1)} %get-tuple-element.37), channel_id=1, source_target_pairs={{0,1},{1,0},{2,3},{3,2},{4,5},{5,4},{6,7},{7,6},{8,9},{9,8},{10,11... | collective-permute-start | bytes 294920 | tf_op jit(solution)/shard_map/ppermute | solution.py:364
  9.6 4.6 %collective-permute-start.4 = (bf16[384,128]{1,0:T(8,128)(2,1)S(1)}, bf16[384,128]{1,0:T(8,128)(2,1)S(1)}, u32[]{:S(2)}, u32[]{:S(2)}) collective-permute-start(bf16[384,128]{1,0:T(8,128)(2,1)S(1)} %get-tuple-element.38), channel_id=1, source_target_pairs={{1,2},{2,1},{9,10},{10,9},{0,8},{8,0},{3,11},{11,3},{5,6},{6,5},{1... | collective-permute-start | bytes 294920 | tf_op jit(solution)/shard_map/ppermute | solution.py:363
  14.3 6.8 %collective-permute-start.5 = (bf16[224,128]{1,0:T(8,128)(2,1)S(1)}, bf16[224,128]{1,0:T(8,128)(2,1)S(1)}, u32[]{:S(2)}, u32[]{:S(2)}) collective-permute-start(bf16[224,128]{1,0:T(8,128)(2,1)S(1)} %pad_maximum_fusion), channel_id=1, source_target_pairs={{0,16},{16,0},{1,17},{17,1},{2,18},{18,2},{3,19},{19,3},{4,20},{20... | collective-permute-start | bytes 172040 | tf_op jit(solution)/shard_map/ppermute | solution.py:343
  24.1 2.4 %collective-permute-start.6 = (bf16[1536,256]{1,0:T(8,128)(2,1)S(1)}, bf16[1536,256]{1,0:T(8,128)(2,1)S(1)}, u32[]{:S(2)}, u32[]{:S(2)}) collective-permute-start(bf16[1536,256]{1,0:T(8,128)(2,1)S(1)} %get-tuple-element.49), channel_id=1, source_target_pairs={{0,4},{4,0},{1,5},{5,1},{2,6},{6,2},{3,7},{7,3},{8,12},{12,8},{9,1... | collective-permute-start | bytes 2359304 | tf_op jit(solution)/shard_map/ppermute | solution.py:343
  42.4 6.6 %collective-permute-start.7 = (bf16[192,256]{1,0:T(8,128)(2,1)S(1)}, bf16[192,256]{1,0:T(8,128)(2,1)S(1)}, u32[]{:S(2)}, u32[]{:S(2)}) collective-permute-start(bf16[192,256]{1,0:T(8,128)(2,1)S(1)} %reduce_sum.12), channel_id=1, source_target_pairs={{0,3},{1,2},{2,1},{3,0},{4,7},{5,6},{6,5},{7,4},{8,11},{9,10},{10,... | collective-permute-start | bytes 294920 | tf_op jit(solution)/shard_map/ppermute | solution.py:535
  62.3 8.7 %collective-permute-start.8 = (bf16[1536,256]{1,0:T(8,128)(2,1)S(1)}, bf16[1536,256]{1,0:T(8,128)(2,1)S(1)}, u32[]{:S(2)}, u32[]{:S(2)}) collective-permute-start(bf16[1536,256]{1,0:T(8,128)(2,1)S(1)} %bitcast.9), channel_id=1, source_target_pairs={{0,4},{4,0},{1,5},{5,1},{2,6},{6,2},{3,7},{7,3},{8,12},{12,8},{9,1... | collective-permute-start | bytes 2359304 | tf_op jit(solution)/shard_map/ppermute | solution.py:343
  62.3 8.7 %collective-permute-start.9 = (bf16[16,32,256]{2,1,0:T(8,128)(2,1)S(1)}, bf16[16,32,256]{2,1,0:T(8,128)(2,1)S(1)}, u32[]{:S(2)}, u32[]{:S(2)}) collective-permute-start(bf16[16,32,256]{2,1,0:T(8,128)(2,1)S(1)} %get-tuple-element.50), channel_id=1, source_target_pairs={{0,16},{16,0},{1,17},{17,1},{2,18},{18,2},{3,19},{19,3},{4,20},{20... | collective-permute-start | bytes 786440 | tf_op jit(solution)/shard_map/ppermute | solution.py:343

commit v5 on v4

--- a/solution.py
+++ b/solution.py
@@ -158,12 +158,14 @@
     spread_taps(slope_two, taps_slope, wide)
     own = half_rows * half_cols
     own_slope = slope_two[1 : half_rows + 1, 0:half_cols].reshape(own, wide).astype(BF16)
-    for row in range(3):
-        window = taps_mid[row + 1 : row + 1 + half_rows, 0:half_cols].reshape(own, 3 * wide)
-        grad = lax.dot_general(window, own_slope, TN, preferred_element_type=F32)
-        for col in range(3):
-            at = (row * 3 + col) * wide
-            flat[at : at + wide, :] = grad[col * wide : (col + 1) * wide].astype(BF16)
+    windows = [
+        taps_mid[row + 1 : row + 1 + half_rows, 0:half_cols].reshape(own, 3 * wide)
+        for row in range(3)
+    ]
+    grad = lax.dot_general(
+        jnp.concatenate(windows, axis=1), own_slope, TN, preferred_element_type=F32
+    )
+    flat[0 : 9 * wide, :] = grad.astype(BF16)
     windows = [
         taps_slope[row : row + half_rows, 0:half_cols].reshape(own, 3 * wide) for row in range(3)
     ]

time: 72.7 us -> 72.6 us (level)
  no operation moved by 1% of the time
where the time goes in v5:
time: 72.6 us; the launch traced here: 72.2 us
  blocking collectives  28.8 us (40%)
  waiting for transfers between devices  17.6 us (24%)
  Pallas kernels  12.9 us (18%)
  starting transfers between devices  11.8 us (16%)
  between operations  0.74 us (1%)
    all_to_all x1, blocking collectives, scatter_sum(): parts = lax.all_to_all(parts, axes, 0, 0, tiled=True)  15.7 us
    all_to_all x1, blocking collectives, gather(): lax.all_to_all(parts, axes, 0, 0, tiled=True).reshape(-1, part.shape[1])  13.2 us
    ppermute x5, waiting for transfers between devices, swap_pairs(): return lax.ppermute(block, axis, [(0, 1), (1, 0)])  9.1 us
    ppermute x1, waiting for transfers between devices, per_device(): theirs = lax.ppermute(part, GX, pairs)  4.71 us
    ppermute x5, starting transfers between devices, swap_pairs(): return lax.ppermute(block, axis, [(0, 1), (1, 0)])  3.69 us
    pallas_call x1, Pallas kernels, forward(): pl.pallas_call(forward_kernel, out_shape=(pltpu.VMEM((half_rows, half_col...  3.67 us
    ppermute x2, starting transfers between devices, swap_neighbours(): odd = lax.ppermute(odd, names, both(far))  3.58 us
    pallas_call x1, Pallas kernels, backward(): pl.pallas_call(functools.partial(backward_kernel, chunk), out_shape=(pltp...  2.85 us
  transfers between devices with their start and end apart: 10, of which 6 were waited for; matrix products, arithmetic and copies ran while one was open for 0% of the time, Pallas kernels for 11%

profile of v5, /device:TPU:0, one launch (start us, length us, event | category | flops | bytes accessed | tf_op | source)
XLA Modules:
  0.0 72.2 jit_solution(11321338316075705127)
XLA Ops:
  0.6 1.0 %shard_map.84 = (bf16[6,64,128]{2,1,0:T(8,128)(2,1)S(1)}, bf16[6,64,128]{2,1,0:T(8,128)(2,1)S(1)}) custom-call(bf16[32,64,128]{2,1,0:T(8,128)(2,1)} %bitcast.11, bf16[16,32,256]{2,1,0:T(8,128)(2,1)} %bitcast.15), custom_call_target="tpu_custom_call" | custom-call | tf_op jit(solution)/shard_map/pallas_call | solution.py:416
  1.7 0.6 collective-permute-start.1
  2.2 2.6 %collective-permute-start.2 = (bf16[6,64,128]{2,1,0:T(8,128)(2,1)S(1)}, bf16[6,64,128]{2,1,0:T(8,128)(2,1)S(1)}, u32[]{:S(2)}, u32[]{:S(2)}) collective-permute-start(bf16[6,64,128]{2,1,0:T(8,128)(2,1)S(1)} %get-tuple-element.32), channel_id=1, source_target_pairs={{4,8},{8,4},{5,9},{9,5},{0,1},{1,0},{12,13},{13,12},{6,10},{10,6},... | collective-permute-start | bytes 294920 | tf_op jit(solution)/shard_map/ppermute | solution.py:365
  4.9 1.5 %collective-permute-start = (bf16[16,32,256]{2,1,0:T(8,128)(2,1)}, bf16[16,32,256]{2,1,0:T(8,128)(2,1)S(1)}, u32[]{:S(2)}, u32[]{:S(2)}) collective-permute-start(bf16[16,32,256]{2,1,0:T(8,128)(2,1)} %bitcast.16), channel_id=1, source_target_pairs={{0,16},{16,0},{1,17},{17,1},{2,18},{18,2},{3,19},{19,3},{4,20},{20... | collective-permute-start | bytes 786440 | tf_op jit(solution)/shard_map/ppermute | solution.py:345
  6.4 1.0 %shard_map.85 = (bf16[32,8,128]{2,1,0:T(8,128)(2,1)S(1)}, bf16[32,8,128]{2,1,0:T(8,128)(2,1)S(1)}, bf16[16,8,256]{2,1,0:T(8,128)(2,1)S(1)}, bf16[16,8,256]{2,1,0:T(8,128)(2,1)S(1)}) custom-call(bf16[32,64,128]{2,1,0:T(8,128)(2,1)} %bitcast.12, bf16[16,32,256]{2,1,0:T(8,128)(2,1)} %bitcast.17), custom_call_target="tpu_custom_call" | custom-call | tf_op jit(solution)/shard_map/pallas_call | solution.py:416
  7.6 2.1 %collective-permute-start.3 = (bf16[384,128]{1,0:T(8,128)(2,1)S(1)}, bf16[384,128]{1,0:T(8,128)(2,1)S(1)}, u32[]{:S(2)}, u32[]{:S(2)}) collective-permute-start(bf16[384,128]{1,0:T(8,128)(2,1)S(1)} %get-tuple-element.37), channel_id=1, source_target_pairs={{0,1},{1,0},{2,3},{3,2},{4,5},{5,4},{6,7},{7,6},{8,9},{9,8},{10,11... | collective-permute-start | bytes 294920 | tf_op jit(solution)/shard_map/ppermute | solution.py:366
  9.6 0.9 %collective-permute-start.4 = (bf16[384,128]{1,0:T(8,128)(2,1)S(1)}, bf16[384,128]{1,0:T(8,128)(2,1)S(1)}, u32[]{:S(2)}, u32[]{:S(2)}) collective-permute-start(bf16[384,128]{1,0:T(8,128)(2,1)S(1)} %get-tuple-element.38), channel_id=1, source_target_pairs={{1,2},{2,1},{9,10},{10,9},{0,8},{8,0},{3,11},{11,3},{5,6},{6,5},{1... | collective-permute-start | bytes 294920 | tf_op jit(solution)/shard_map/ppermute | solution.py:365
  10.6 2.2 %collective-permute-done.3.cols_even = bf16[384,128]{1,0:T(8,128)(2,1)S(1)} collective-permute-done((bf16[384,128]{1,0:T(8,128)(2,1)S(1)}, bf16[384,128]{1,0:T(8,128)(2,1)S(1)}, u32[]{:S(2)}, u32[]{:S(2)}) %collective-permute-start.3) | collective-permute-done | bytes 98336 | tf_op jit(solution)/shard_map/ppermute | solution.py:366
  12.8 1.5 %collective-permute-done.4.cols_odd = bf16[384,128]{1,0:T(8,128)(2,1)S(1)} collective-permute-done((bf16[384,128]{1,0:T(8,128)(2,1)S(1)}, bf16[384,128]{1,0:T(8,128)(2,1)S(1)}, u32[]{:S(2)}, u32[]{:S(2)}) %collective-permute-start.4) | collective-permute-done | bytes 98336 | tf_op jit(solution)/shard_map/ppermute | solution.py:365
  14.3 1.6 %collective-permute-start.5 = (bf16[224,128]{1,0:T(8,128)(2,1)S(1)}, bf16[224,128]{1,0:T(8,128)(2,1)S(1)}, u32[]{:S(2)}, u32[]{:S(2)}) collective-permute-start(bf16[224,128]{1,0:T(8,128)(2,1)S(1)} %pad_maximum_fusion), channel_id=1, source_target_pairs={{0,16},{16,0},{1,17},{17,1},{2,18},{18,2},{3,19},{19,3},{4,20},{20... | collective-permute-start | bytes 172040 | tf_op jit(solution)/shard_map/ppermute | solution.py:345
  15.8 1.6 %shard_map.87 = (bf16[32,64,128]{2,1,0:T(8,128)(2,1)S(1)}, bf16[3,3,128,128]{3,2,1,0:T(8,128)(2,1)S(1)}, bf16[128,256]{1,0:T(8,128)(2,1)S(1)}, bf16[3,3,256,256]{3,2,1,0:T(8,128)(2,1)S(1)}) custom-call(bf16[32,64,128]{2,1,0:T(8,128)(2,1)} %bitcast.13, bf16[3,3,128,128]{3,2,1,0:T(8,128)(2,1)} %refs_1_.1, bf16[128,256]{1,0:T(8,128)(2,1)} %refs_2_.1, ...), custom_call_target="tpu_custom_call" | custom-call | tf_op jit(solution)/shard_map/pallas_call | solution.py:475
  17.4 3.7 %shard_map.88 = (bf16[16,32,256]{2,1,0:T(8,128)(2,1)S(1)}, bf16[42,80,384]{2,1,0:T(8,128)(2,1)S(1)}, f32[20,80,256]{2,1,0:T(8,128)S(1)}, bf16[20,40,768]{2,1,0:T...) custom-call(bf16[32,64,128]{2,1,0:T(8,128)(2,1)S(1)} %get-tuple-element.39.tile, ...), custom_call_target="tpu_custom_call" | custom-call | tf_op jit(solution)/shard_map/pallas_call | solution.py:224
  21.1 2.8 %shard_map.89 = (bf16[1536,256]{1,0:T(8,128)(2,1)S(1)}, bf16[1536,256]{1,0:T(8,128)(2,1)S(1)}) custom-call(bf16[16,32,256]{2,1,0:T(8,128)(2,1)S(1)} %collective-permute-done.theirs, bf16[224,128]{1,0:T(8,128)(2,1)S(1)} %collective-permute-done.5.ring, bf16[42,80,384]{2,1,0:T(8,128)(2,1)S(1)} %get-tuple-element.43.taps_one, ...), custom_call_target="tpu_custom_call" | custom-call | tf_op jit(solution)/shard_map/pallas_call | solution.py:251
  24.0 2.3 %collective-permute-done.6 = bf16[1536,256]{1,0:T(8,128)(2,1)S(1)} collective-permute-done((bf16[1536,256]{1,0:T(8,128)(2,1)S(1)}, bf16[1536,256]{1,0:T(8,128)(2,1)S(1)}, u32[]{:S(2)}, u32[]{:S(2)}) %collective-permute-start.6) | collective-permute-done | bytes 786464 | tf_op jit(solution)/shard_map/ppermute | solution.py:345
  26.3 0.2 add_convert_fusion
  26.5 15.7 %all_to_all.10 = bf16[8,192,256]{2,1,0:T(8,128)(2,1)S(1)} all-to-all(bf16[8,192,256]{2,1,0:T(8,128)(2,1)S(1)} %bitcast.14), channel_id=1, replica_groups=mesh['section'=2,'gy_hi'=2,'core'=2,'gx_hi'=2,'gx_lo'=2] {'section','gy_..., dimensions={0} | all-to-all | bytes 1572864 | tf_op jit(solution)/shard_map/all_to_all | solution.py:500
  42.2 0.1 reduce_sum.12
  42.3 1.9 %collective-permute-start.7 = (bf16[192,256]{1,0:T(8,128)(2,1)S(1)}, bf16[192,256]{1,0:T(8,128)(2,1)S(1)}, u32[]{:S(2)}, u32[]{:S(2)}) collective-permute-start(bf16[192,256]{1,0:T(8,128)(2,1)S(1)} %reduce_sum.12), channel_id=1, source_target_pairs={{0,3},{1,2},{2,1},{3,0},{4,7},{5,6},{6,5},{7,4},{8,11},{9,10},{10,... | collective-permute-start | bytes 294920 | tf_op jit(solution)/shard_map/ppermute | solution.py:537
  44.2 4.7 %collective-permute-done.7 = bf16[192,256]{1,0:T(8,128)(2,1)S(1)} collective-permute-done((bf16[192,256]{1,0:T(8,128)(2,1)S(1)}, bf16[192,256]{1,0:T(8,128)(2,1)S(1)}, u32[]{:S(2)}, u32[]{:S(2)}) %collective-permute-start.7) | collective-permute-done | bytes 98336 | tf_op jit(solution)/shard_map/ppermute | solution.py:537
  49.0 13.2 %all_to_all.11 = bf16[8,192,256]{2,1,0:T(8,128)(2,1)S(1)} all-to-all(bf16[8,192,256]{2,1,0:T(8,128)(2,1)S(1)} %broadcast_in_dim.4), channel_id=1, replica_groups=mesh['section'=2,'gy_hi'=2,'core'=2,'gx_hi'=2,'gx_lo'=2] {'section','gy_..., dimensions={0} | all-to-all | bytes 1572864 | tf_op jit(solution)/shard_map/all_to_all | solution.py:506
  62.2 0.6 collective-permute-start.9
  62.7 1.3 %shard_map.90 = (f32[3,3,128,128]{3,2,1,0:T(8,128)}, f32[128,256]{1,0:T(8,128)}, f32[3,3,256,256]{3,2,1,0:T(8,128)}) custom-call(bf16[1536,256]{1,0:T(8,128)(2,1)S(1)} %bitcast.10), custom_call_target="tpu_custom_call" | custom-call | tf_op jit(solution)/shard_map/pallas_call | solution.py:330
  64.1 6.8 %collective-permute-done.9.features = bf16[16,32,256]{2,1,0:T(8,128)(2,1)S(1)} collective-permute-done((bf16[16,32,256]{2,1,0:T(8,128)(2,1)S(1)}, bf16[16,32,256]{2,1,0:T(8,128)(2,1)S(1)}, u32[]{:S(2)}, u32[]{:S(2)}) %collective-permute-start.9) | collective-permute-done | bytes 262176 | tf_op jit(solution)/shard_map/ppermute | solution.py:345
  70.9 1.4 %shard_map.91 = (bf16[16,32,256]{2,1,0:T(8,128)(2,1)}, f32[3,3,128,128]{3,2,1,0:T(8,128)}, f32[128,256]{1,0:T(8,128)}, f32[3,3,256,256]{3,2,1,0:T(8,128)}) custom-call(bf16[1536,256]{1,0:T(8,128)(2,1)S(1)} %collective-permute-done.8.source, ...), custom_call_target="tpu_custom_call", output_to_operand_aliasing={{1}: (2, {}), {2}: (3, {}), {3}: (4, {})} | custom-call | tf_op jit(solution)/shard_map/pallas_call | solution.py:330
  (15 shorter events, 0.4 us)
Async XLA Ops:
  1.7 5.7 %collective-permute-start.1 = (bf16[6,64,128]{2,1,0:T(8,128)(2,1)S(1)}, bf16[6,64,128]{2,1,0:T(8,128)(2,1)S(1)}, u32[]{:S(2)}, u32[]{:S(2)}) collective-permute-start(bf16[6,64,128]{2,1,0:T(8,128)(2,1)S(1)} %get-tuple-element.31), channel_id=1, source_target_pairs={{0,4},{4,0},{8,12},{12,8},{1,5},{5,1},{9,13},{13,9},{2,6},{6,2},{1... | collective-permute-start | bytes 294920 | tf_op jit(solution)/shard_map/ppermute | solution.py:366
  2.2 5.2 %collective-permute-start.2 = (bf16[6,64,128]{2,1,0:T(8,128)(2,1)S(1)}, bf16[6,64,128]{2,1,0:T(8,128)(2,1)S(1)}, u32[]{:S(2)}, u32[]{:S(2)}) collective-permute-start(bf16[6,64,128]{2,1,0:T(8,128)(2,1)S(1)} %get-tuple-element.32), channel_id=1, source_target_pairs={{4,8},{8,4},{5,9},{9,5},{0,1},{1,0},{12,13},{13,12},{6,10},{10,6},... | collective-permute-start | bytes 294920 | tf_op jit(solution)/shard_map/ppermute | solution.py:365
  4.9 16.2 %collective-permute-start = (bf16[16,32,256]{2,1,0:T(8,128)(2,1)}, bf16[16,32,256]{2,1,0:T(8,128)(2,1)S(1)}, u32[]{:S(2)}, u32[]{:S(2)}) collective-permute-start(bf16[16,32,256]{2,1,0:T(8,128)(2,1)} %bitcast.16), channel_id=1, source_target_pairs={{0,16},{16,0},{1,17},{17,1},{2,18},{18,2},{3,19},{19,3},{4,20},{20... | collective-permute-start | bytes 786440 | tf_op jit(solution)/shard_map/ppermute | solution.py:345
  7.6 5.2 %collective-permute-start.3 = (bf16[384,128]{1,0:T(8,128)(2,1)S(1)}, bf16[384,128]{1,0:T(8,128)(2,1)S(1)}, u32[]{:S(2)}, u32[]{:S(2)}) collective-permute-start(bf16[384,128]{1,0:T(8,128)(2,1)S(1)} %get-tuple-element.37), channel_id=1, source_target_pairs={{0,1},{1,0},{2,3},{3,2},{4,5},{5,4},{6,7},{7,6},{8,9},{9,8},{10,11... | collective-permute-start | bytes 294920 | tf_op jit(solution)/shard_map/ppermute | solution.py:366
  9.6 4.6 %collective-permute-start.4 = (bf16[384,128]{1,0:T(8,128)(2,1)S(1)}, bf16[384,128]{1,0:T(8,128)(2,1)S(1)}, u32[]{:S(2)}, u32[]{:S(2)}) collective-permute-start(bf16[384,128]{1,0:T(8,128)(2,1)S(1)} %get-tuple-element.38), channel_id=1, source_target_pairs={{1,2},{2,1},{9,10},{10,9},{0,8},{8,0},{3,11},{11,3},{5,6},{6,5},{1... | collective-permute-start | bytes 294920 | tf_op jit(solution)/shard_map/ppermute | solution.py:365
  14.3 6.8 %collective-permute-start.5 = (bf16[224,128]{1,0:T(8,128)(2,1)S(1)}, bf16[224,128]{1,0:T(8,128)(2,1)S(1)}, u32[]{:S(2)}, u32[]{:S(2)}) collective-permute-start(bf16[224,128]{1,0:T(8,128)(2,1)S(1)} %pad_maximum_fusion), channel_id=1, source_target_pairs={{0,16},{16,0},{1,17},{17,1},{2,18},{18,2},{3,19},{19,3},{4,20},{20... | collective-permute-start | bytes 172040 | tf_op jit(solution)/shard_map/ppermute | solution.py:345
  24.0 2.4 %collective-permute-start.6 = (bf16[1536,256]{1,0:T(8,128)(2,1)S(1)}, bf16[1536,256]{1,0:T(8,128)(2,1)S(1)}, u32[]{:S(2)}, u32[]{:S(2)}) collective-permute-start(bf16[1536,256]{1,0:T(8,128)(2,1)S(1)} %get-tuple-element.49), channel_id=1, source_target_pairs={{0,4},{4,0},{1,5},{5,1},{2,6},{6,2},{3,7},{7,3},{8,12},{12,8},{9,1... | collective-permute-start | bytes 2359304 | tf_op jit(solution)/shard_map/ppermute | solution.py:345
  42.3 6.6 %collective-permute-start.7 = (bf16[192,256]{1,0:T(8,128)(2,1)S(1)}, bf16[192,256]{1,0:T(8,128)(2,1)S(1)}, u32[]{:S(2)}, u32[]{:S(2)}) collective-permute-start(bf16[192,256]{1,0:T(8,128)(2,1)S(1)} %reduce_sum.12), channel_id=1, source_target_pairs={{0,3},{1,2},{2,1},{3,0},{4,7},{5,6},{6,5},{7,4},{8,11},{9,10},{10,... | collective-permute-start | bytes 294920 | tf_op jit(solution)/shard_map/ppermute | solution.py:537
  62.2 8.7 %collective-permute-start.8 = (bf16[1536,256]{1,0:T(8,128)(2,1)S(1)}, bf16[1536,256]{1,0:T(8,128)(2,1)S(1)}, u32[]{:S(2)}, u32[]{:S(2)}) collective-permute-start(bf16[1536,256]{1,0:T(8,128)(2,1)S(1)} %bitcast.9), channel_id=1, source_target_pairs={{0,4},{4,0},{1,5},{5,1},{2,6},{6,2},{3,7},{7,3},{8,12},{12,8},{9,1... | collective-permute-start | bytes 2359304 | tf_op jit(solution)/shard_map/ppermute | solution.py:345
  62.2 8.7 %collective-permute-start.9 = (bf16[16,32,256]{2,1,0:T(8,128)(2,1)S(1)}, bf16[16,32,256]{2,1,0:T(8,128)(2,1)S(1)}, u32[]{:S(2)}, u32[]{:S(2)}) collective-permute-start(bf16[16,32,256]{2,1,0:T(8,128)(2,1)S(1)} %get-tuple-element.50), channel_id=1, source_target_pairs={{0,16},{16,0},{1,17},{17,1},{2,18},{18,2},{3,19},{19,3},{4,20},{20... | collective-permute-start | bytes 786440 | tf_op jit(solution)/shard_map/ppermute | solution.py:345
